TPU v7x, 128 devices: a whole 4x4x4 slice. The times are simulated.
128 devices in a mesh: geo: 8 (over x, core), dist: 16 (over z, y).
Axes of the slice: x: 4, y: 4, z: 4, core: 2. Of those that a mesh axis runs over, the one named last changes fastest.
Arguments:
- estimates: bfloat16 [6144, 7424], P(('geo', 'dist')), may hold values from -4 to 4
- factors: bfloat16 [6144, 7424], P(('geo', 'dist')), may hold values from -0.625 to 0.625
- variances: bfloat16 [6144, 116], P(('geo', 'dist')), may hold values from 0.019897461 to 0.5
- intersection_tracts: int32 [2048, 32], P('dist'), may hold values from 0 to 6143, as said below
- intersection_weights: int32 [2048, 32], P('dist'), may hold values from 1 to 256
Outputs:
- marginal: float32 [2048, 7424], P('dist')
- covariance: float32 [2048, 13456], P('dist')
Inputs may be any that keep to these rules, and one draw needn't show every extreme that they name: `intersection_tracts`: each district's intersections are 32 different tracts among 64 consecutive ones, counted cyclically over the region.
All inputs are finite; a program needn't handle non-finite values.
Results may differ from a plain program's by a relative error of at most 0.0003.
Values may be sent and summed in bfloat16 or wider, within the bound.
A program may use at most 128 MiB of HBM per device.

v0:
```python
import jax
import jax.numpy as jnp
from jax import lax
from jax.sharding import PartitionSpec as P


def assemble(est_sum, fac_sum, var_sum):
    count = est_sum.shape[0]
    ages = var_sum.shape[1]
    shaped = fac_sum.reshape(count, ages, fac_sum.shape[1] // ages)
    outer = jnp.einsum("dik,djk->dij", shaped, shaped, precision=lax.Precision.HIGHEST)
    outer = outer + var_sum[:, :, None] * jnp.eye(ages, dtype=jnp.float32)[None, :, :]
    return (est_sum, outer.reshape(count, ages * ages))


def shards(estimates, factors, variances, intersection_tracts, intersection_weights):
    geo_index = lax.axis_index("geo")
    block = estimates.shape[0] * lax.axis_size("dist")
    local_ids = intersection_tracts - geo_index * block
    positions = jnp.arange(block, dtype=jnp.int32)
    onehot = (local_ids[:, :, None] == positions[None, None, :]).astype(jnp.float32)
    share = intersection_weights.astype(jnp.float32) / 256.0
    weight_mat = jnp.sum(onehot * share[:, :, None], axis=1).astype(jnp.bfloat16)
    square_mat = jnp.sum(onehot * (share * share)[:, :, None], axis=1)
    est_new = jnp.dot(
        weight_mat,
        lax.all_gather(estimates, "dist", axis=0, tiled=True),
        preferred_element_type=jnp.float32,
    )
    fac_new = jnp.dot(
        weight_mat,
        lax.all_gather(factors, "dist", axis=0, tiled=True),
        preferred_element_type=jnp.float32,
    )
    var_new = jnp.dot(
        square_mat,
        lax.all_gather(variances, "dist", axis=0, tiled=True).astype(jnp.float32),
        precision=lax.Precision.HIGHEST,
    )
    est_sum, fac_sum, var_sum = lax.psum((est_new, fac_new, var_new), "geo")
    return assemble(est_sum, fac_sum, var_sum)


def solution(mesh):
    return jax.shard_map(
        shards,
        mesh=mesh,
        in_specs=(
            P(("geo", "dist"), None),
            P(("geo", "dist"), None),
            P(("geo", "dist"), None),
            P("dist", None),
            P("dist", None),
        ),
        out_specs=(P("dist", None), P("dist", None)),
        check_vma=False,
    )
```

profile of v0, /device:TPU:1, one launch (start us, length us, event | category | flops | bytes accessed | tf_op | source)
XLA Modules:
  0.0 340.1 jit_solution(11527298273313712709)
XLA Ops:
  7.2 0.0 all-gather.5.cloned.1.call-start
  7.2 0.7 all-gather.5.cloned.1.call-update
  7.9 0.0 all-gather.3.cloned.1.call-start
  7.9 0.7 all-gather.3.cloned.1.call-update
  8.6 0.0 all-reduce.3.cloned.1.call-start
  8.7 0.7 convert_multiply_fusion
  9.4 0.1 copy.24
  9.5 0.7 broadcast_subtract_fusion
  10.2 0.1 copy.20
  10.3 0.1 copy.21
  10.4 13.2 %select_reduce_fusion = (f32[128,768]{1,0:T(8,128)S(1)}, bf16[128,768]{1,0:T(8,128)(2,1)S(1)}) fusion(f32[128,32]{1,0:T(8,128)S(1)} %copy.24, s32[128,32]{1,0:T(8,128)S(1)} %copy.20, f32[128,32]{1,0:T(8,128)S(1)} %copy.21), kind=kLoop, calls=%fused_computation | loop fusion | flops 15532032 | bytes 638976 | tf_op jit(solution)/shard_map/reduce_sum | solution.py:24
  23.6 74.5 %all-gather.5.cloned.1.call-done = bf16[768,7424]{1,0:T(8,128)(2,1)} async-done(((bf16[48,7424]{1,0:T(8,128)(2,1)}), bf16[768,7424]{1,0:T(8,128)(2,1)}) %all-gather.5.cloned.1.call-update) | async-done | bytes 11403280 | tf_op jit(solution)/shard_map/all_gather | solution.py:32
  98.1 10.6 %fusion.7 = f32[128,7424]{0,1:T(8,128)} fusion(bf16[128,768]{1,0:T(8,128)(2,1)S(1)} %get-tuple-element.5, bf16[768,7424]{1,0:T(8,128)(2,1)} %all-gather.5.cloned.1.call-done), kind=kOutput, calls=%fused_computation.14 | convolution fusion | flops 1459617792 | bytes 15400960 | tf_op jit(solution)/shard_map/dot_general | solution.py:30
  108.7 5.4 %copy.23 = f32[128,116,64]{1,2,0:T(8,128)} copy(f32[128,116,64]{0,2,1:T(8,128)} %bitcast.9) | data formatting | bytes 7602176 | tf_op jit(solution)/shard_map/reshape | solution.py:10
  114.2 0.0 copy-start
  114.2 70.4 %all-gather.3.cloned.1.call-done = bf16[768,7424]{1,0:T(8,128)(2,1)} async-done(((bf16[48,7424]{1,0:T(8,128)(2,1)}), bf16[768,7424]{1,0:T(8,128)(2,1)}) %all-gather.3.cloned.1.call-update) | async-done | bytes 11403280 | tf_op jit(solution)/shard_map/all_gather | solution.py:27
  184.5 7.8 %fusion.8 = f32[128,7424]{1,0:T(8,128)} fusion(bf16[128,768]{1,0:T(8,128)(2,1)S(1)} %get-tuple-element.5, bf16[768,7424]{1,0:T(8,128)(2,1)} %all-gather.3.cloned.1.call-done), kind=kOutput, calls=%fused_computation.15 | convolution fusion | flops 1459617792 | bytes 15400960 | tf_op jit(solution)/shard_map/dot_general | solution.py:25
  192.3 0.0 all-reduce.3.cloned.1.call-update
  192.3 0.0 copy-done
  192.3 19.1 %all_gather.11 = bf16[768,116]{1,0:T(8,128)(2,1)S(1)} all-gather(bf16[48,116]{1,0:T(8,128)(2,1)S(1)} %copy-done), channel_id=1, replica_groups=mesh['geo'=8,'dist'=16] {'dist'}, dimensions={0}, use_global_device_ids=true | all-gather | bytes 189312 | tf_op jit(solution)/shard_map/all_gather | solution.py:37
  211.5 0.4 fusion.6
  211.9 27.8 %psum.23 = f32[128,116]{0,1:T(8,128)S(1)} all-reduce(f32[128,116]{0,1:T(8,128)S(1)} %fusion.6), channel_id=1, replica_groups=mesh['geo'=8,'dist'=16] {'geo'}, use_global_device_ids=true, to_apply=%region_4.0 | all-reduce | flops 14848 | bytes 118784 | tf_op jit(solution)/shard_map/psum | solution.py:40
  239.6 0.1 copy.25
  239.7 52.9 %all-reduce.3.cloned.1.call-done = (f32[128,7424]{1,0:T(8,128)}, f32[128,116,64]{1,2,0:T(8,128)}) async-done(((f32[128,7424]{1,0:T(8,128)}, f32[128,116,64]{1,2,0:T(8,128)}), (f32[128,7424]{1,0:T(8,128)}, f32[128,116,64]{1,2,0:T(8,128)})) %all-reduce.3.cloned.1.call-update) | async-done | bytes 7602192 | tf_op jit(solution)/shard_map/psum | solution.py:40
  292.6 20.0 %multiply_add_fusion = f32[128,116,116]{2,1,0:T(8,128)} fusion(f32[116,116]{1,0:T(8,128)S(1)} %fusion.4, f32[128,116]{1,0:T(8,128)S(1)} %copy.25, f32[128,116,64]{1,2,0:T(8,128)} %get-tuple-element.7), kind=kOutput, calls=%fused_computation.3 | convolution fusion | flops 1326223360 | bytes 10803776 | tf_op jit(solution)/shard_map/dik,djk->dij/dot_general | solution.py:11
  312.6 8.5 %reshape.24 = f32[128,13456]{1,0:T(8,128)} reshape(f32[128,116,116]{2,1,0:T(8,128)} %multiply_add_fusion) | data formatting | bytes 13778944 | tf_op jit(solution)/shard_map/reshape | solution.py:13
  321.2 8.2 %copy.28 = f32[128,13456]{0,1:T(8,128)} copy(f32[128,13456]{1,0:T(8,128)} %reshape.24) | data formatting | bytes 13778944 | tf_op jit(solution)/shard_map/reshape | solution.py:13
  329.4 4.2 %copy.31 = f32[128,7424]{1,0:T(8,128)} copy(f32[128,7424]{1,0:T(8,128)} %get-tuple-element.10) | data formatting | bytes 7602176
  (1 shorter events, 0.0 us)
Async XLA Ops:
  7.2 90.9 %all-gather.5.cloned.1.call-start = ((), (), s32[]{:S(2)}) async-start(), calls=%async_computation.1 | async-start | bytes 12115968 | tf_op jit(solution)/shard_map/all_gather | solution.py:32
  7.9 176.6 %all-gather.3.cloned.1.call-start = ((), (), s32[]{:S(2)}) async-start(), calls=%async_computation | async-start | bytes 12115968 | tf_op jit(solution)/shard_map/all_gather | solution.py:27
  8.6 284.0 %all-reduce.3.cloned.1.call-start = ((), (), s32[]{:S(2)}) async-start(), calls=%async_computation.2 | async-start | bytes 15990784 | tf_op jit(solution)/shard_map/psum | solution.py:40
  114.2 78.2 %copy-start = (bf16[48,116]{1,0:T(8,128)(2,1)S(1)}, bf16[48,116]{1,0:T(8,128)(2,1)}, u32[]{:S(2)}) copy-start(bf16[48,116]{1,0:T(8,128)(2,1)} %param.7) | copy-start | bytes 33412
Sparse Core Ops, SparseCore 0:
  10.1 87.8 all-gather.4
  100.2 84.2 all-gather.2
  192.5 100.1 all-reduce.2
where the time goes:
time: 341 us; the launch traced here: 340 us
  waiting for transfers between devices  199 us (58%)
  blocking collectives  46.9 us (14%)
  matrix products  38.8 us (11%)
  local copies, waits for them, and re-layouts  26.8 us (8%)
  other arithmetic  14.6 us (4%)
  between operations  13.8 us (4%)
    all_gather x1, waiting for transfers between devices, shards(): lax.all_gather(factors, 'dist', axis=0, tiled=True)  74.5 us
    all_gather x1, waiting for transfers between devices, shards(): lax.all_gather(estimates, 'dist', axis=0, tiled=True)  70.4 us
    psum x1, waiting for transfers between devices, shards(): est_sum, fac_sum, var_sum = lax.psum((est_new, fac_new, var_new), 'geo')  52.9 us
    psum x1, blocking collectives, shards(): est_sum, fac_sum, var_sum = lax.psum((est_new, fac_new, var_new), 'geo')  27.8 us
    dot_general x1, matrix products, assemble(): jnp.einsum('dik,djk->dij', shaped, shaped, precision=lax.Precision.HIGHEST)  20 us
    all_gather x1, blocking collectives, shards(): lax.all_gather(variances, 'dist', axis=0, tiled=True).astype(jnp.float32)  19.1 us
    reshape x2, local copies, waits for them, and re-layouts, assemble(): return (est_sum, outer.reshape(count, ages * ages))  16.8 us
    reduce_sum x1, other arithmetic, shards(): square_mat = jnp.sum(onehot * (share * share)[:, :, None], axis=1)  13.2 us
  transfers between devices with their start and end apart: 3, of which 3 were waited for; matrix products, arithmetic and copies ran while one was open for 9% of the time, Pallas kernels for 0%

commit v1 on v0

v1 whole, which is shorter than its diff:
```python
import jax
import jax.numpy as jnp
from jax import lax
from jax.experimental import pallas as pl
from jax.experimental.pallas import tpu as pltpu
from jax.sharding import PartitionSpec as P

MESH = pl.DeviceIdType.MESH
GEO, DIST = 8, 16
DEVICES = GEO * DIST
LANES = 128
ROWS = 48
TRACTS = ROWS * DEVICES
DB = 128
INTER = 32
TABLE_TILES = 58
HI, LO = 2 * TABLE_TILES, 2 * TABLE_TILES + 1
TILES = 2 * TABLE_TILES + 2
PER_GEO = 15
SLOTS = GEO * PER_GEO
CODE_ROWS = DB + 16
STEPS = 32000.0
AGES, RANK = 116, 64


def owner_tile(g, d):
    return g * PER_GEO + d


def has_tile(g, d):
    return jnp.logical_and(d < PER_GEO, owner_tile(g, d) < TILES)


def sums_kernel(idx, wgt, est, fac, var, out,
                pk, varp, table, weight, block, coded,
                local_sem, pk_send, pk_recv, row_send, row_recv,
                tile_send, slot_recv, right_send, left_send, core_send):
    g = lax.axis_index("geo")
    d = lax.axis_index("dist")
    me = g * DIST + d
    tau = owner_tile(g, d)
    mine = has_tile(g, d)

    packed = idx[...] * 512 + wgt[...]
    pk[d] = jnp.transpose(packed)

    def pk_copy(slot, to):
        return pltpu.make_async_remote_copy(
            src_ref=pk.at[slot], dst_ref=pk.at[slot], send_sem=pk_send.at[to],
            recv_sem=pk_recv.at[slot], device_id=(g, to), device_id_type=MESH)

    def pk_start(s, _):
        pk_copy(d, lax.rem(d + s, DIST)).start()
        return 0
    lax.fori_loop(1, DIST, pk_start, 0)

    varp[...] = jnp.zeros_like(varp)
    varp[:, 0:AGES] = var[...]

    def row_copy(ge, de, src, tile_ref_cols):
        e = ge * DIST + de
        return pltpu.make_async_remote_copy(
            src_ref=src.at[:, tile_ref_cols],
            dst_ref=table.at[pl.ds(pl.multiple_of(me * ROWS, 16), ROWS), :],
            send_sem=row_send.at[e], recv_sem=row_recv.at[me],
            device_id=(ge, de), device_id_type=MESH)

    def own_copy(src, cols):
        return pltpu.make_async_copy(
            src.at[:, cols],
            table.at[pl.ds(pl.multiple_of(me * ROWS, 16), ROWS), :], local_sem.at[0])

    def for_tile(t, action):
        @pl.when(t < TABLE_TILES)
        def _():
            action(est, pl.ds(pl.multiple_of(t * LANES, LANES), LANES))

        @pl.when(jnp.logical_and(t >= TABLE_TILES, t < HI))
        def _():
            action(fac, pl.ds(pl.multiple_of((t - TABLE_TILES) * LANES, LANES), LANES))

        @pl.when(jnp.logical_and(t >= HI, t < TILES))
        def _():
            action(varp, pl.ds(0, LANES))

    def row_start(s, _):
        e = lax.rem(me + s, DEVICES)
        ge, de = lax.div(e, DIST), lax.rem(e, DIST)

        @pl.when(de < PER_GEO)
        def _():
            for_tile(owner_tile(ge, de), lambda src, cols: row_copy(ge, de, src, cols).start())
        return 0

    @pl.when(mine)
    def _():
        for_tile(tau, lambda src, cols: own_copy(src, cols).start())
    lax.fori_loop(1, DEVICES, row_start, 0)

    lane = lax.broadcasted_iota(jnp.int32, (DB, LANES), 1)
    residue = lax.broadcasted_iota(jnp.int32, (64, DB), 0)

    def weights_of(s, _):
        dd = lax.rem(d + s, DIST)

        @pl.when(s > 0)
        def _():
            pk_copy(dd, d).wait_recv()
        entries = pk[dd]
        res = lax.shift_right_logical(entries, 9) & 63
        val = (lax.shift_right_logical(entries, 15) * 512) + (entries & 511)
        acc = jnp.zeros((64, DB), jnp.int32)
        for k in range(INTER):
            acc = jnp.where(residue == res[k:k + 1, :], val[k:k + 1, :], acc)
        both = jnp.transpose(jnp.concatenate([acc, acc], axis=0))
        w = both & 511
        square = w * w
        w = jnp.where(tau == HI, lax.shift_right_logical(square, 8),
                      jnp.where(tau == LO, square & 255, w))
        b = lax.shift_right_logical(both, 9) - jnp.where(lane >= 64, 1, 0)
        weight[dd] = (w.astype(jnp.float32) * (1.0 / 256.0)).astype(jnp.bfloat16)
        block[dd] = b.astype(jnp.float32).astype(jnp.bfloat16)
        return 0
    lax.fori_loop(0, DIST, weights_of, 0)

    @pl.when(mine)
    def _():
        def row_wait(s, _):
            e = lax.rem(me + DEVICES - s, DEVICES)
            at = table.at[pl.ds(pl.multiple_of(e * ROWS, 16), ROWS), :]
            pltpu.make_async_remote_copy(
                src_ref=at, dst_ref=at, send_sem=row_send.at[e], recv_sem=row_recv.at[e],
                device_id=(g, d), device_id_type=MESH).wait_recv()
            return 0
        for_tile(tau, lambda src, cols: own_copy(src, cols).wait())
        lax.fori_loop(1, DEVICES, row_wait, 0)

    x, c = lax.div(g, 2), lax.rem(g, 2)
    g_right = lax.rem(x + 1, 4) * 2 + c
    g_left = lax.rem(x + 3, 4) * 2 + c
    g_far = lax.rem(x + 2, 4) * 2 + c
    g_core = x * 2 + (1 - c)

    def slot_copy(slot, send_sem, to_g):
        return pltpu.make_async_remote_copy(
            src_ref=out.at[slot], dst_ref=out.at[slot], send_sem=send_sem,
            recv_sem=slot_recv.at[slot], device_id=(to_g, d), device_id_type=MESH)

    def tile_copy(dd):
        return pltpu.make_async_remote_copy(
            src_ref=coded.at[dd], dst_ref=out.at[tau], send_sem=tile_send.at[dd],
            recv_sem=slot_recv.at[tau], device_id=(g, dd), device_id_type=MESH)

    def own_tile_copy():
        return pltpu.make_async_copy(coded.at[d], out.at[tau], local_sem.at[1])

    def compute(dd):
        w = weight[dd]
        b = block[dd]
        acc = jnp.zeros((DB, LANES), jnp.float32)
        zero = jnp.zeros_like(w)
        for step in range(TRACTS // 256):
            parts = []
            for h in range(2):
                at = float(2 * (2 * step + h))
                parts.append(jnp.where(b == jnp.full_like(b, at), w, zero))
            acc = acc + jnp.dot(jnp.concatenate(parts, axis=1), table[step * 256:(step + 1) * 256, :],
                                preferred_element_type=jnp.float32)
        top = jnp.maximum(jnp.max(jnp.abs(acc), axis=0, keepdims=True), 1e-30)
        e = jnp.ceil(jnp.log2(top))
        code = jnp.round(acc * (STEPS / jnp.exp2(e)))
        coded[dd, 0:DB, :] = code.astype(jnp.int32).astype(jnp.int16)
        coded[dd, DB:CODE_ROWS, :] = jnp.broadcast_to(e, (16, LANES)).astype(jnp.int32).astype(jnp.int16)

    def slot_of(gg, s):
        dd = lax.rem(d + DIST - s, DIST)
        return dd, owner_tile(gg, dd), has_tile(gg, dd)

    def from_dist(s):
        dd, slot, there = slot_of(g, s)

        @pl.when(there)
        def _():
            @pl.when(s == 0)
            def _():
                own_tile_copy().wait()

            @pl.when(s > 0)
            def _():
                slot_copy(slot, tile_send.at[0], g_right).wait_recv()
            slot_copy(slot, right_send.at[0, dd], g_right).start()
            slot_copy(slot, left_send.at[0, dd], g_left).start()
            slot_copy(slot, core_send.at[0, dd], g_core).start()

    def from_side(gg, to_g, sems, parity, n, s):
        dd, slot, there = slot_of(gg, s)

        @pl.when(there)
        def _():
            slot_copy(slot, tile_send.at[0], g_right).wait_recv()

            @pl.when(lax.rem(dd, 2) == parity)
            def _():
                slot_copy(slot, sems.at[1, dd], to_g).start()
            slot_copy(slot, core_send.at[n, dd], g_core).start()

    def from_far(s):
        dd, slot, there = slot_of(g_far, s)

        @pl.when(there)
        def _():
            slot_copy(slot, tile_send.at[0], g_right).wait_recv()
            slot_copy(slot, core_send.at[3, dd], g_core).start()

    def at_step(t, lag, body):
        s = t - lag

        @pl.when(jnp.logical_and(s >= 0, s < DIST))
        def _():
            body(s)

    def send_step(s):
        dd = lax.rem(d + s, DIST)

        @pl.when(mine)
        def _():
            compute(dd)

            @pl.when(s > 0)
            def _():
                tile_copy(dd).start()

            @pl.when(s == 0)
            def _():
                own_tile_copy().start()

    def round_of(t, _):
        at_step(t, 0, send_step)
        at_step(t, 1, from_dist)
        at_step(t, 3, lambda s: from_side(g_left, g_right, right_send, 0, 1, s))
        at_step(t, 3, lambda s: from_side(g_right, g_left, left_send, 1, 2, s))
        at_step(t, 5, from_far)
        return 0
    lax.fori_loop(0, DIST + 5, round_of, 0)

    def from_core(s, _):
        for gg in (g, g_left, g_right, g_far):
            other = lax.div(gg, 2) * 2 + (1 - c)
            _, slot, there = slot_of(other, s)

            @pl.when(there)
            def _():
                slot_copy(slot, tile_send.at[0], g_right).wait_recv()
        return 0
    lax.fori_loop(0, DIST, from_core, 0)

    def sent(s, _):
        dd, slot, there = slot_of(g, s)

        @pl.when(jnp.logical_and(mine, s > 0))
        def _():
            tile_copy(dd).wait_send()

        @pl.when(s > 0)
        def _():
            pk_copy(d, dd).wait_send()

        @pl.when(there)
        def _():
            slot_copy(slot, right_send.at[0, dd], g_right).wait_send()
            slot_copy(slot, left_send.at[0, dd], g_left).wait_send()
            slot_copy(slot, core_send.at[0, dd], g_core).wait_send()
        for gg, to_g, sems, parity, n in ((g_left, g_right, right_send, 0, 1), (g_right, g_left, left_send, 1, 2)):
            dd, slot, there = slot_of(gg, s)

            @pl.when(there)
            def _():
                @pl.when(lax.rem(dd, 2) == parity)
                def _():
                    slot_copy(slot, sems.at[1, dd], to_g).wait_send()
                slot_copy(slot, core_send.at[n, dd], g_core).wait_send()
        dd, slot, there = slot_of(g_far, s)

        @pl.when(there)
        def _():
            slot_copy(slot, core_send.at[3, dd], g_core).wait_send()
        return 0
    lax.fori_loop(0, DIST, sent, 0)

    def rows_sent(s, _):
        e = lax.rem(me + s, DEVICES)
        ge, de = lax.div(e, DIST), lax.rem(e, DIST)

        @pl.when(has_tile(ge, de))
        def _():
            row_copy(ge, de, varp, pl.ds(0, LANES)).wait_send()
        return 0
    lax.fori_loop(1, DEVICES, rows_sent, 0)


def tile_sums(idx, wgt, est, fac, var):
    vmem = pl.BlockSpec(memory_space=pltpu.VMEM)
    hbm = pl.BlockSpec(memory_space=pl.ANY)
    dma = pltpu.SemaphoreType.DMA
    return pl.pallas_call(
        sums_kernel,
        out_shape=jax.ShapeDtypeStruct((SLOTS, CODE_ROWS, LANES), jnp.int16),
        in_specs=[vmem, vmem, hbm, hbm, vmem],
        out_specs=hbm,
        scratch_shapes=[
            pltpu.VMEM((DIST, INTER, DB), jnp.int32),
            pltpu.VMEM((ROWS, LANES), jnp.bfloat16),
            pltpu.VMEM((TRACTS, LANES), jnp.bfloat16),
            pltpu.VMEM((DIST, DB, LANES), jnp.bfloat16),
            pltpu.VMEM((DIST, DB, LANES), jnp.bfloat16),
            pltpu.VMEM((DIST, CODE_ROWS, LANES), jnp.int16),
            dma((2,)), dma((DIST,)), dma((DIST,)), dma((DEVICES,)), dma((DEVICES,)),
            dma((DIST,)), dma((SLOTS,)), dma((2, DIST)), dma((2, DIST)), dma((4, DIST)),
        ],
        compiler_params=pltpu.CompilerParams(has_side_effects=True, vmem_limit_bytes=48 * 2**20),
        name="tile_sums",
    )(idx, wgt, est, fac, var)


GROUP = 8
CROWS = 120


def blocks_kernel(slots_hbm, marg_hbm, cov_hbm, slots, loading, marg, noise, paired, outer, flat, in_sem, marg_sem, cov_sem):
    def fetch(i):
        start, size = ((TABLE_TILES, SLOTS - TABLE_TILES), (0, TABLE_TILES))[i]
        return pltpu.make_async_copy(slots_hbm.at[pl.ds(start, size)], slots.at[pl.ds(start, size)], in_sem.at[i])
    fetch(0).start()
    fetch(1).start()
    fetch(0).wait()

    def decode(slot):
        code = slots[slot, 0:DB, :].astype(jnp.int32).astype(jnp.float32)
        e = slots[slot, DB:CODE_ROWS, :].astype(jnp.int32).astype(jnp.float32)
        return code * (jnp.exp2(e[0:1, :]) * (1.0 / STEPS))

    noise[...] = decode(HI) + decode(LO) * (1.0 / 256.0)

    def load_tile(t, _):
        loading[pl.ds(pl.multiple_of(t * DB, DB), DB), :] = decode(TABLE_TILES + t)
        return 0
    lax.fori_loop(0, TABLE_TILES, load_tile, 0)

    fetch(1).wait()
    for t in range(TABLE_TILES):
        marg[:, t * LANES:(t + 1) * LANES] = decode(t)
    out_marg = pltpu.make_async_copy(marg, marg_hbm, marg_sem)
    out_marg.start()

    paired[...] = jnp.zeros_like(paired)
    lane_row = lax.broadcasted_iota(jnp.int32, (TABLE_TILES, LANES), 1)
    lane_full = lax.broadcasted_iota(jnp.int32, (LANES, LANES), 1)
    lane = lax.broadcasted_iota(jnp.int32, (GROUP, LANES), 1)

    def cov_copy(grp, at):
        return pltpu.make_async_copy(flat.at[at], cov_hbm.at[pl.ds(pl.multiple_of(grp * GROUP, GROUP), GROUP), :], cov_sem.at[at])

    def group(grp, _):
        at = lax.rem(grp, 2)

        @pl.when(grp >= 2)
        def _():
            cov_copy(grp - 2, at).wait()
        for k in range(GROUP):
            rows = loading[pl.ds(grp * GROUP + k, TABLE_TILES, stride=DB), :]
            turned = pltpu.roll(rows, RANK, axis=1)
            low = lane_row < RANK
            paired[k, pl.ds(0, TABLE_TILES, stride=2), :] = jnp.where(low, rows, turned)
            paired[k, pl.ds(1, TABLE_TILES, stride=2), :] = jnp.where(low, turned, rows)
        for k in range(GROUP):
            full = paired[k]
            hi = full.astype(jnp.bfloat16)
            lo = (full - hi.astype(jnp.float32)).astype(jnp.bfloat16)
            mixed = jnp.where(lane_full < RANK, hi, lo)
            left = jnp.concatenate([mixed, mixed], axis=1)
            right = jnp.concatenate([hi, lo], axis=1)
            product = lax.dot_general(left, right, (((1,), (1,)), ((), ())), preferred_element_type=jnp.float32)
            outer[k * CROWS:(k + 1) * CROWS, :] = product[0:CROWS, :]
        extra = noise[pl.ds(pl.multiple_of(grp * GROUP, GROUP), GROUP), :]
        current = None
        for i in range(AGES):
            row = outer[pl.ds(i, GROUP, stride=CROWS), :]
            row = row + jnp.where(lane == i, extra, 0.0)
            tile, off = divmod(AGES * i, LANES)
            turned = pltpu.roll(row, off, axis=1) if off else row
            current = jnp.where(lane < off, current, turned) if off else turned
            if off + AGES >= LANES:
                flat[at, :, tile * LANES:(tile + 1) * LANES] = current
                current = turned
        done = (AGES * AGES // LANES) * LANES
        flat[at, :, done:AGES * AGES] = current[:, 0:AGES * AGES - done]
        cov_copy(grp, at).start()
        return 0
    lax.fori_loop(0, DB // GROUP, group, 0)
    cov_copy(DB // GROUP - 2, 0).wait()
    cov_copy(DB // GROUP - 1, 1).wait()
    out_marg.wait()


def blocks(slots):
    hbm = pl.BlockSpec(memory_space=pl.ANY)
    dma = pltpu.SemaphoreType.DMA
    return pl.pallas_call(
        blocks_kernel,
        out_shape=(jax.ShapeDtypeStruct((DB, TABLE_TILES * LANES), jnp.float32),
                   jax.ShapeDtypeStruct((DB, AGES * AGES), jnp.float32)),
        in_specs=[hbm],
        out_specs=(hbm, hbm),
        scratch_shapes=[
            pltpu.VMEM((SLOTS, CODE_ROWS, LANES), jnp.int16),
            pltpu.VMEM((TABLE_TILES * DB, LANES), jnp.float32),
            pltpu.VMEM((DB, TABLE_TILES * LANES), jnp.float32),
            pltpu.VMEM((DB, LANES), jnp.float32),
            pltpu.VMEM((GROUP, LANES, LANES), jnp.float32),
            pltpu.VMEM((GROUP * CROWS, LANES), jnp.float32),
            pltpu.VMEM((2, GROUP, AGES * AGES), jnp.float32),
            dma((2,)), dma(()), dma((2,)),
        ],
        compiler_params=pltpu.CompilerParams(vmem_limit_bytes=48 * 2**20),
        name="district_blocks",
    )(slots)


def shards(estimates, factors, variances, intersection_tracts, intersection_weights):
    slots = tile_sums(intersection_tracts, intersection_weights, estimates, factors, variances)
    return blocks(slots)


def solution(mesh):
    return jax.shard_map(
        shards,
        mesh=mesh,
        in_specs=(
            P(("geo", "dist"), None),
            P(("geo", "dist"), None),
            P(("geo", "dist"), None),
            P("dist", None),
            P("dist", None),
        ),
        out_specs=(P("dist", None), P("dist", None)),
        check_vma=False,
    )
```

time: 341 us -> 121 us (0.35)
  the two profiles are of different devices: /device:TPU:1 before, /device:TPU:25 now
where the time goes in v1:
time: 121 us; the launch traced here: 120 us
  Pallas kernels  107 us (88%)
  local copies, waits for them, and re-layouts  12.8 us (11%)
    pallas_call x1, Pallas kernels, tile_sums(): pl.pallas_call(sums_kernel, out_shape=jax.ShapeDtypeStruct((SLOTS, CODE_R...  92.6 us
    pallas_call x1, Pallas kernels, blocks(): pl.pallas_call(blocks_kernel, out_shape=(jax.ShapeDtypeStruct((DB, TABLE_...  14.2 us
    pallas_call x1, local copies, waits for them, and re-layouts, blocks(): pl.pallas_call(blocks_kernel, out_shape=(jax.ShapeDtypeStruct((DB, TABLE_...  8.21 us
    unnamed x8, local copies, waits for them, and re-layouts  4.55 us

profile of v1, /device:TPU:25, one launch (start us, length us, event | category | flops | bytes accessed | tf_op | source)
XLA Modules:
  0.0 120.2 jit_solution(1377464720145035697)
XLA Ops:
  0.6 0.8 copy.7.idx
  1.4 0.8 copy.8.wgt
  2.3 0.0 copy-start
  2.3 1.1 copy-done
  3.4 0.0 copy-start.1
  3.4 1.1 copy-done.1
  4.5 0.0 copy-start.2
  4.5 0.7 copy-done.2
  5.2 92.6 %tile_sums.1.slots_hbm = s16[120,144,128]{2,1,0:T(8,128)(2,1)S(1)} custom-call(s32[128,32]{1,0:T(8,128)S(1)} %copy.7.idx, s32[128,32]{1,0:T(8,128)S(1)} %copy.8.wgt, bf16[48,7424]{1,0:T(8,128)(2,1)S(1)} %copy-done, bf16[48,7424]{1,0:T(8,128)(2,1)S(1)} %copy-done.1, bf16[48,116]{1,0:T(8,128)(2,1)S(1)} %copy-done.2), custom_call_target="tpu_custom_call" | custom-call | tf_op jit(solution)/shard_map/tile_sums/pallas_call | solution.py:305
  97.8 14.2 %district_blocks.1 = (f32[128,7424]{1,0:T(8,128)}, f32[128,13456]{1,0:T(8,128)}) custom-call(s16[120,144,128]{2,1,0:T(8,128)(2,1)S(1)} %tile_sums.1.slots_hbm), custom_call_target="tpu_custom_call" | custom-call | tf_op jit(solution)/shard_map/district_blocks/pallas_call | solution.py:408
  112.0 8.2 %copy.9 = f32[128,13456]{0,1:T(8,128)} copy(f32[128,13456]{1,0:T(8,128)} %get-tuple-element.3) | data formatting | bytes 13778944 | tf_op jit(solution)/shard_map/district_blocks/pallas_call | solution.py:408
Async XLA Ops:
  2.3 1.1 copy-start
  3.4 1.1 copy-start.1
  4.5 0.7 copy-start.2

commit v2 on v0

v2 whole, which is shorter than its diff:
```python
import jax
import jax.numpy as jnp
from jax import lax
from jax.experimental import pallas as pl
from jax.experimental.pallas import tpu as pltpu
from jax.sharding import PartitionSpec as P

MESH = pl.DeviceIdType.MESH
GEO, DIST = 8, 16
DEVICES = GEO * DIST
LANES = 128
ROWS = 48
TRACTS = ROWS * DEVICES
BLOCK = ROWS * DIST
DB = 128
INTER = 32
TABLE_TILES = 58
HI, LO = 2 * TABLE_TILES, 2 * TABLE_TILES + 1
PER_GEO = 15
SLOTS = GEO * PER_GEO
CODE_ROWS = DB + 8
STEPS = 32000.0
AGES, RANK = 116, 64
SIDE_LAG, FAR_LAG = 4, 8


def sums_kernel(idx, wgt, est, fac, var, out,
                pk, varp, table, weight, block, sums, coded,
                ready, own_sem, pk_send, pk_recv, row_send, row_recv,
                tile_send, slot_recv, right_send, left_send, core_send, core_recv):
    g = lax.axis_index("geo")
    d = lax.axis_index("dist")
    me = g * DIST + d
    tau = g * PER_GEO + d
    mine = d < PER_GEO
    x, c = lax.div(g, 2), lax.rem(g, 2)
    g_right = lax.rem(x + 1, 4) * 2 + c
    g_left = lax.rem(x + 3, 4) * 2 + c
    g_far = lax.rem(x + 2, 4) * 2 + c
    g_core = x * 2 + (1 - c)

    barrier = pltpu.get_barrier_semaphore()
    for s in range(1, DIST):
        pl.semaphore_signal(barrier, inc=1, device_id=(g, lax.rem(d + s, DIST)), device_id_type=MESH)
    for s in range(1, GEO):
        pl.semaphore_signal(barrier, inc=1, device_id=(lax.rem(g + s, GEO), d), device_id_type=MESH)

    pk[d] = idx[...] * 512 + wgt[...]
    varp[...] = jnp.zeros_like(varp)
    varp[:, 0:AGES] = var[...]

    my_rows = table.at[pl.ds(pl.multiple_of(me * ROWS, 16), ROWS), :]

    def row_copy(ge, de, src, cols):
        return pltpu.make_async_remote_copy(
            src_ref=src.at[:, cols], dst_ref=my_rows, send_sem=row_send.at[0],
            recv_sem=row_recv.at[g], device_id=(ge, de), device_id_type=MESH)

    def for_tile(t, action):
        @pl.when(t < TABLE_TILES)
        def _():
            action(est, pl.ds(pl.multiple_of(t * LANES, LANES), LANES))

        @pl.when(jnp.logical_and(t >= TABLE_TILES, t < HI))
        def _():
            action(fac, pl.ds(pl.multiple_of((t - TABLE_TILES) * LANES, LANES), LANES))

        @pl.when(t >= HI)
        def _():
            action(varp, pl.ds(0, LANES))

    @pl.when(mine)
    def _():
        for_tile(tau, lambda src, cols: pltpu.make_async_copy(src.at[:, cols], my_rows, row_recv.at[g]).start())

    pl.semaphore_wait(barrier, DIST - 1 + GEO - 1)
    for s in range(1, GEO):
        pl.semaphore_signal(ready, inc=1, device_id=(lax.rem(g + s, GEO), d), device_id_type=MESH)

    def pk_copy(slot, to):
        return pltpu.make_async_remote_copy(
            src_ref=pk.at[slot], dst_ref=pk.at[slot], send_sem=pk_send.at[0],
            recv_sem=pk_recv.at[0], device_id=(g, to), device_id_type=MESH)

    def pk_start(s, _):
        pk_copy(d, lax.rem(d + s, DIST)).start()
        return 0
    lax.fori_loop(1, DIST, pk_start, 0)

    def rows_to(r, ks):
        ge = lax.rem(g + r, GEO)

        def one(k, _):
            de = lax.rem(d + k, DIST)

            @pl.when(de < PER_GEO)
            def _():
                for_tile(ge * PER_GEO + de, lambda src, cols: row_copy(ge, de, src, cols).start())
            return 0
        lax.fori_loop(ks, DIST, one, 0)
        return 0
    rows_to(0, 1)
    pl.semaphore_wait(ready, GEO - 1)
    lax.fori_loop(1, GEO, lambda r, _: rows_to(r, 0), 0)

    others = pk.at[pl.ds(0, DIST - 1)]
    pltpu.make_async_copy(others, others, pk_recv.at[0]).wait()
    lane = lax.broadcasted_iota(jnp.int32, (DB, LANES), 1)
    residue = lax.broadcasted_iota(jnp.int32, (64, DB), 0)

    def weights_of(dd, _):
        entries = pk[dd]
        res = lax.shift_right_logical(entries, 9) & 63
        val = (lax.shift_right_logical(entries, 15) * 512) + (entries & 511)
        acc = jnp.zeros((64, DB), jnp.int32)
        for k in range(INTER):
            acc = jnp.where(residue == res[k:k + 1, :], val[k:k + 1, :], acc)
        both = jnp.transpose(jnp.concatenate([acc, acc], axis=0))
        w = both & 511
        square = w * w
        w = jnp.where(tau == HI, lax.shift_right_logical(square, 8),
                      jnp.where(tau == LO, square & 255, w))
        b = lax.shift_right_logical(both, 9) - jnp.where(lane >= 64, 1, 0)
        weight[dd] = (w.astype(jnp.float32) * (1.0 / 256.0)).astype(jnp.bfloat16)
        block[dd] = b.astype(jnp.float32).astype(jnp.bfloat16)
        return 0
    lax.fori_loop(0, DIST, weights_of, 0)

    many = 4

    def product(q, gb):
        w = weight[pl.ds(q * many, many)].reshape(many * DB, LANES)
        b = block[pl.ds(q * many, many)].reshape(many * DB, LANES)
        zero = jnp.zeros_like(w)
        total = None
        for step in range(BLOCK // 256):
            parts = []
            for h in range(2):
                at = (2 * (gb * (BLOCK // LANES) + 2 * step + h)).astype(jnp.float32).astype(jnp.bfloat16)
                parts.append(jnp.where(b == at, w, zero))
            rows = table[pl.ds(pl.multiple_of(gb * BLOCK + step * 256, 256), 256), :]
            part = jnp.dot(jnp.concatenate(parts, axis=1), rows, preferred_element_type=jnp.float32)
            total = part if total is None else total + part
        return total.reshape(many, DB, LANES)

    def tile_copy(dd):
        return pltpu.make_async_remote_copy(
            src_ref=coded.at[dd], dst_ref=out.at[tau], send_sem=tile_send.at[0],
            recv_sem=slot_recv.at[tau], device_id=(g, dd), device_id_type=MESH)

    def own_tile_copy():
        return pltpu.make_async_copy(coded.at[d], out.at[tau], own_sem)

    def encode(dd):
        total = sums[dd]
        top = jnp.maximum(jnp.max(jnp.abs(total), axis=0, keepdims=True), 1e-30)
        e = jnp.ceil(jnp.log2(top))
        code = jnp.round(total * (STEPS / jnp.exp2(e)))
        coded[dd, 0:DB, :] = code.astype(jnp.int32).astype(jnp.int16)
        coded[dd, DB:CODE_ROWS, :] = jnp.broadcast_to(e, (8, LANES)).astype(jnp.int32).astype(jnp.int16)

    @pl.when(mine)
    def _():
        def block_of(r, _):
            gb = lax.rem(g + GEO - r, GEO)
            rows = table.at[pl.ds(pl.multiple_of(gb * BLOCK, 256), BLOCK), :]
            pltpu.make_async_copy(rows, rows, row_recv.at[gb]).wait()

            def quarter(i, _):
                q = lax.rem(lax.div(d, many) + i, DIST // many)

                @pl.when(r == 0)
                def _():
                    sums[pl.ds(q * many, many)] = product(q, gb)

                @pl.when(r > 0)
                def _():
                    sums[pl.ds(q * many, many)] += product(q, gb)

                @pl.when(r == GEO - 1)
                def _():
                    for k in range(many):
                        dd = q * many + lax.rem(lax.rem(d, many) + k, many)
                        encode(dd)

                        @pl.when(dd != d)
                        def _():
                            tile_copy(dd).start()

                        @pl.when(dd == d)
                        def _():
                            own_tile_copy().start()
                return 0
            lax.fori_loop(0, DIST // many, quarter, 0)
            return 0
        lax.fori_loop(0, GEO, block_of, 0)

    def slot_copy(slot, send_sem, recv_sem, to_g):
        return pltpu.make_async_remote_copy(
            src_ref=out.at[slot], dst_ref=out.at[slot], send_sem=send_sem,
            recv_sem=recv_sem, device_id=(to_g, d), device_id_type=MESH)

    def arrived(slot):
        pltpu.make_async_copy(out.at[slot], out.at[slot], slot_recv.at[slot]).wait()

    def to_core(slot):
        slot_copy(slot, core_send.at[0], core_recv.at[0], g_core).start()

    def source(j):
        i, k = lax.div(j, many), lax.rem(j, many)
        return (lax.rem(lax.div(d, many) + DIST // many - i, DIST // many) * many
                + lax.rem(lax.rem(d, many) + many - k, many))

    def from_dist(j):
        dd = source(j)
        slot = g * PER_GEO + dd

        @pl.when(dd < PER_GEO)
        def _():
            @pl.when(dd == d)
            def _():
                own_tile_copy().wait()

            @pl.when(dd != d)
            def _():
                arrived(slot)
            slot_copy(slot, right_send.at[0], slot_recv.at[slot], g_right).start()
            slot_copy(slot, left_send.at[0], slot_recv.at[slot], g_left).start()
            to_core(slot)

    def from_sides(j):
        dd = source(j)
        from_left, from_right = g_left * PER_GEO + dd, g_right * PER_GEO + dd

        @pl.when(dd < PER_GEO)
        def _():
            arrived(from_left)

            @pl.when(lax.rem(dd, 2) == 0)
            def _():
                slot_copy(from_left, right_send.at[1], slot_recv.at[from_left], g_right).start()
            to_core(from_left)
            arrived(from_right)

            @pl.when(lax.rem(dd, 2) == 1)
            def _():
                slot_copy(from_right, left_send.at[1], slot_recv.at[from_right], g_left).start()
            to_core(from_right)

    def from_far(j):
        dd = source(j)

        @pl.when(dd < PER_GEO)
        def _():
            arrived(g_far * PER_GEO + dd)
            to_core(g_far * PER_GEO + dd)

    def at_step(t, lag, body):
        j = t - lag

        @pl.when(jnp.logical_and(j >= 0, j < DIST))
        def _():
            body(j)

    def round_of(t, _):
        at_step(t, 0, from_dist)
        at_step(t, SIDE_LAG, from_sides)
        at_step(t, FAR_LAG, from_far)
        return 0
    lax.fori_loop(0, DIST + FAR_LAG, round_of, 0)

    def wait_slots(sem, n):
        ref = out.at[pl.ds(0, n)]
        pltpu.make_async_copy(ref, ref, sem).wait()
    wait_slots(core_recv.at[0], 4 * PER_GEO)
    wait_slots(core_send.at[0], 4 * PER_GEO)
    wait_slots(right_send.at[0], PER_GEO)
    wait_slots(left_send.at[0], PER_GEO)
    wait_slots(right_send.at[1], 8)
    wait_slots(left_send.at[1], 7)
    pltpu.make_async_copy(others, others, pk_send.at[0]).wait()

    @pl.when(mine)
    def _():
        wait_slots(tile_send.at[0], DIST - 1)
        ref = table.at[pl.ds(0, (SLOTS - 1) * ROWS), :]
        pltpu.make_async_copy(ref, ref, row_send.at[0]).wait()

    @pl.when(jnp.logical_not(mine))
    def _():
        ref = table.at[pl.ds(0, SLOTS * ROWS), :]
        pltpu.make_async_copy(ref, ref, row_send.at[0]).wait()


def tile_sums(idx, wgt, est, fac, var):
    vmem = pl.BlockSpec(memory_space=pltpu.VMEM)
    hbm = pl.BlockSpec(memory_space=pltpu.MemorySpace.HBM)
    dma = pltpu.SemaphoreType.DMA
    return pl.pallas_call(
        sums_kernel,
        out_shape=jax.ShapeDtypeStruct((SLOTS, CODE_ROWS, LANES), jnp.int16),
        in_specs=[vmem, vmem, hbm, hbm, vmem],
        out_specs=vmem,
        scratch_shapes=[
            pltpu.VMEM((DIST, INTER, DB), jnp.int32),
            pltpu.VMEM((ROWS, LANES), jnp.bfloat16),
            pltpu.VMEM((TRACTS, LANES), jnp.bfloat16),
            pltpu.VMEM((DIST, DB, LANES), jnp.bfloat16),
            pltpu.VMEM((DIST, DB, LANES), jnp.bfloat16),
            pltpu.VMEM((DIST, DB, LANES), jnp.float32),
            pltpu.VMEM((DIST, CODE_ROWS, LANES), jnp.int16),
            pltpu.SemaphoreType.REGULAR, dma(()), dma((1,)), dma((1,)), dma((1,)), dma((GEO,)),
            dma((1,)), dma((SLOTS,)), dma((2,)), dma((2,)), dma((1,)), dma((1,)),
        ],
        compiler_params=pltpu.CompilerParams(has_side_effects=True, collective_id=0, vmem_limit_bytes=40 * 2**20),
        name="tile_sums",
    )(idx, wgt, est, fac, var)


GROUP = 8
CROWS = 120
CHUNK = 4


def blocks_kernel(slots, marg_hbm, cov_hbm, loading, marg, noise, paired, outer, flat, marg_sem, cov_sem):
    def decode(slot):
        code = slots[slot, 0:DB, :].astype(jnp.int32).astype(jnp.float32)
        e = slots[slot, DB:CODE_ROWS, :].astype(jnp.int32).astype(jnp.float32)
        return code * (jnp.exp2(e[0:1, :]) * (1.0 / STEPS))

    for t in range(TABLE_TILES):
        marg[:, t * LANES:(t + 1) * LANES] = decode(t)
    out_marg = pltpu.make_async_copy(marg, marg_hbm, marg_sem)
    out_marg.start()

    noise[...] = jnp.transpose(decode(HI) + decode(LO) * (1.0 / 256.0))

    def load_tile(t, _):
        loading[pl.ds(pl.multiple_of(t * DB, DB), DB), :] = decode(TABLE_TILES + t)
        return 0
    lax.fori_loop(0, TABLE_TILES, load_tile, 0)

    paired[...] = jnp.zeros_like(paired)
    lane_row = lax.broadcasted_iota(jnp.int32, (TABLE_TILES, LANES), 1)
    lane_full = lax.broadcasted_iota(jnp.int32, (LANES, LANES), 1)
    sub = lax.broadcasted_iota(jnp.int32, (LANES, LANES), 0)

    def group(grp, _):
        for k in range(GROUP):
            rows = loading[pl.ds(grp * GROUP + k, TABLE_TILES, stride=DB), :]
            turned = pltpu.roll(rows, RANK, axis=1)
            low = lane_row < RANK
            paired[k, pl.ds(0, TABLE_TILES, stride=2), :] = jnp.where(low, rows, turned)
            paired[k, pl.ds(1, TABLE_TILES, stride=2), :] = jnp.where(low, turned, rows)
        for k in range(GROUP):
            full = paired[k]
            hi = full.astype(jnp.bfloat16)
            lo = (full - hi.astype(jnp.float32)).astype(jnp.bfloat16)
            mixed = jnp.where(lane_full < RANK, hi, lo)
            left = jnp.concatenate([mixed, mixed], axis=1)
            right = jnp.concatenate([hi, lo], axis=1)
            product = lax.dot_general(left, right, (((1,), (1,)), ((), ())), preferred_element_type=jnp.float32)
            outer[pl.ds(pl.multiple_of((grp * GROUP + k) * CROWS, 8), CROWS), :] = product[0:CROWS, :]
        return 0
    lax.fori_loop(0, DB // GROUP, group, 0)

    span = CHUNK * AGES

    def cov_copy(n):
        rows = pl.ds(pl.multiple_of(n * span, 8), span)
        return pltpu.make_async_copy(flat.at[rows, :], cov_hbm.at[rows, :], cov_sem)

    def ages(n, _):
        for pair in range(CHUNK // 2):
            halves = []
            for h in range(2):
                i = n * CHUNK + pair * 2 + h
                block = jnp.transpose(outer[pl.ds(i, DB, stride=CROWS), :])
                block = block + jnp.where(sub == i, noise[pl.ds(i, 1), :], 0.0)
                halves.append(block[0:AGES, :])
            flat[pl.ds(pl.multiple_of(n * span + pair * 2 * AGES, 8), 2 * AGES), :] = jnp.concatenate(halves, axis=0)
        cov_copy(n).start()
        return 0
    lax.fori_loop(0, AGES // CHUNK, ages, 0)
    pltpu.make_async_copy(flat, cov_hbm, cov_sem).wait()
    out_marg.wait()


def blocks(slots):
    vmem = pl.BlockSpec(memory_space=pltpu.VMEM)
    hbm = pl.BlockSpec(memory_space=pltpu.MemorySpace.HBM)
    dma = pltpu.SemaphoreType.DMA
    marg, cov = pl.pallas_call(
        blocks_kernel,
        out_shape=(jax.ShapeDtypeStruct((DB, TABLE_TILES * LANES), jnp.float32),
                   jax.ShapeDtypeStruct((AGES * AGES, DB), jnp.float32)),
        in_specs=[vmem],
        out_specs=(hbm, hbm),
        scratch_shapes=[
            pltpu.VMEM((TABLE_TILES * DB, LANES), jnp.float32),
            pltpu.VMEM((DB, TABLE_TILES * LANES), jnp.float32),
            pltpu.VMEM((DB, LANES), jnp.float32),
            pltpu.VMEM((GROUP, LANES, LANES), jnp.float32),
            pltpu.VMEM((DB * CROWS, LANES), jnp.float32),
            pltpu.VMEM((AGES * AGES, DB), jnp.float32),
            dma(()), dma(()),
        ],
        compiler_params=pltpu.CompilerParams(vmem_limit_bytes=48 * 2**20),
        name="district_blocks",
    )(slots)
    return marg, cov.T


def shards(estimates, factors, variances, intersection_tracts, intersection_weights):
    slots = tile_sums(intersection_tracts.T, intersection_weights.T, estimates, factors, variances)
    return blocks(slots)


def solution(mesh):
    return jax.shard_map(
        shards,
        mesh=mesh,
        in_specs=(
            P(("geo", "dist"), None),
            P(("geo", "dist"), None),
            P(("geo", "dist"), None),
            P("dist", None),
            P("dist", None),
        ),
        out_specs=(P("dist", None), P("dist", None)),
        check_vma=False,
    )
```

time: 341 us -> 86.7 us (0.25)
  waiting for transfers between devices: 199 us -> 0 us
  Pallas kernels: 0 us -> 81.4 us
  blocking collectives: 46.9 us -> 0 us
  matrix products: 38.8 us -> 0 us
  local copies, waits for them, and re-layouts: 26.8 us -> 4.35 us
  other arithmetic: 14.6 us -> 0 us
  between operations: 13.8 us -> 0.65 us
    all_gather x2 -> x0, waiting for transfers between devices: 145 us -> none  [the longest x1 74.5 us: shards(): lax.all_gather(factors, 'dist', axis=0, tiled=True)]
    pallas_call x0 -> x2, Pallas kernels: none -> 81.4 us  [the longest x1 68.2 us: tile_sums(): pl.pallas_call(sums_kernel, out_shape=jax.ShapeDtypeStruct((SLOTS, CODE_R...]
    psum x1 -> x0, waiting for transfers between devices: 52.9 us -> none  [shards(): est_sum, fac_sum, var_sum = lax.psum((est_new, fac_new, var_new), 'geo')]
    dot_general x4 -> x0, matrix products: 38.8 us -> none  [the longest x1 20 us: assemble(): jnp.einsum('dik,djk->dij', shaped, shaped, precision=lax.Precision.HIGHEST)]
    psum x1 -> x0, blocking collectives: 27.8 us -> none  [shards(): est_sum, fac_sum, var_sum = lax.psum((est_new, fac_new, var_new), 'geo')]
    reshape x3 -> x0, local copies, waits for them, and re-layouts: 22.2 us -> none  [the longest x2 16.8 us: assemble(): return (est_sum, outer.reshape(count, ages * ages))]
    all_gather x1 -> x0, blocking collectives: 19.1 us -> none  [shards(): lax.all_gather(variances, 'dist', axis=0, tiled=True).astype(jnp.float32)]
    reduce_sum x1 -> x0, other arithmetic: 13.2 us -> none  [shards(): square_mat = jnp.sum(onehot * (share * share)[:, :, None], axis=1)]
  transfers between devices with their start and end apart: 3 -> 0, of which waited for: 3 -> 0; matrix products, arithmetic and copies ran while one was open for 9% -> 0% of each run, Pallas kernels for 0% -> 0%
where the time goes in v2:
time: 86.7 us; the launch traced here: 86.4 us
  Pallas kernels  81.4 us (94%)
  local copies, waits for them, and re-layouts  4.35 us (5%)
    pallas_call x1, Pallas kernels, tile_sums(): pl.pallas_call(sums_kernel, out_shape=jax.ShapeDtypeStruct((SLOTS, CODE_R...  68.2 us
    pallas_call x1, Pallas kernels, blocks(): pl.pallas_call(blocks_kernel, out_shape=(jax.ShapeDtypeStruct((DB, TABLE_...  13.2 us
    unnamed x10, local copies, waits for them, and re-layouts  4.35 us

profile of v2, /device:TPU:1, one launch (start us, length us, event | category | flops | bytes accessed | tf_op | source)
XLA Modules:
  0.0 86.4 jit_solution(1183512672479594256)
XLA Ops:
  0.6 0.0 copy-start
  0.6 1.1 %copy-done = bf16[48,7424]{1,0:T(8,128)(2,1)S(1)} copy-done((bf16[48,7424]{1,0:T(8,128)(2,1)S(1)}, bf16[48,7424]{1,0:T(8,128)(2,1)}, u32[]{:S(2)}) %copy-start) | copy-done | bytes 712728
  1.7 0.0 copy-start.1
  1.7 1.1 %copy-done.1 = bf16[48,7424]{1,0:T(8,128)(2,1)S(1)} copy-done((bf16[48,7424]{1,0:T(8,128)(2,1)S(1)}, bf16[48,7424]{1,0:T(8,128)(2,1)}, u32[]{:S(2)}) %copy-start.1) | copy-done | bytes 712728
  2.8 0.0 copy-start.2
  2.8 0.7 copy-done.2
  3.6 0.0 copy-start.3
  3.6 0.7 copy-done.3
  4.3 0.0 copy-start.4
  4.3 0.7 copy-done.4
  5.0 68.2 %tile_sums.1.slots = s16[120,136,128]{2,1,0:T(8,128)(2,1)S(1)} custom-call(s32[32,128]{1,0:T(8,128)S(1)} %bitcast.3, s32[32,128]{1,0:T(8,128)S(1)} %bitcast.4, bf16[48,7424]{1,0:T(8,128)(2,1)S(1)} %copy-done, bf16[48,7424]{1,0:T(8,128)(2,1)S(1)} %copy-done.1, bf16[48,116]{1,0:T(8,128)(2,1)S(1)} %copy-done.4), custom_call_target="tpu_custom_call" | custom-call | tf_op jit(solution)/shard_map/tile_sums/pallas_call | solution.py:299
  73.2 13.2 %district_blocks.1 = (f32[128,7424]{1,0:T(8,128)}, f32[13456,128]{1,0:T(8,128)}) custom-call(s16[120,136,128]{2,1,0:T(8,128)(2,1)S(1)} %tile_sums.1.slots), custom_call_target="tpu_custom_call" | custom-call | tf_op jit(solution)/shard_map/district_blocks/pallas_call | solution.py:393
Async XLA Ops:
  0.6 1.1 %copy-start = (bf16[48,7424]{1,0:T(8,128)(2,1)S(1)}, bf16[48,7424]{1,0:T(8,128)(2,1)}, u32[]{:S(2)}) copy-start(bf16[48,7424]{1,0:T(8,128)(2,1)} %est.1) | copy-start | bytes 2138116
  1.7 1.1 %copy-start.1 = (bf16[48,7424]{1,0:T(8,128)(2,1)S(1)}, bf16[48,7424]{1,0:T(8,128)(2,1)}, u32[]{:S(2)}) copy-start(bf16[48,7424]{1,0:T(8,128)(2,1)} %fac.1) | copy-start | bytes 2138116
  2.8 0.7 copy-start.2
  3.6 0.7 copy-start.3
  4.3 0.7 copy-start.4

commit v3 on v2

--- a/solution.py
+++ b/solution.py
@@ -14,26 +14,54 @@
 BLOCK = ROWS * DIST
 DB = 128
 INTER = 32
+WIDE = 2 * LANES
 TABLE_TILES = 58
-HI, LO = 2 * TABLE_TILES, 2 * TABLE_TILES + 1
+PAIRS = TABLE_TILES // 2
+HI, LO = PAIRS, PAIRS + 1
 PER_GEO = 15
+HALF = DIST // 2
 SLOTS = GEO * PER_GEO
 CODE_ROWS = DB + 8
 STEPS = 32000.0
 AGES, RANK = 116, 64
-SIDE_LAG, FAR_LAG = 4, 8
-
-
-def sums_kernel(idx, wgt, est, fac, var, out,
+SIDE_LAG, FAR_LAG = 8, 14
+AHEAD = 4
+
+
+def even_pair(x, d):
+    return x * 8 + lax.div(d, 2)
+
+
+def odd_pair(x, d):
+    return x * 7 + lax.div(d, 2)
+
+
+def factor_slot(t):
+    f = t // 2
+    return ((f // 8) * 2 + t % 2) * PER_GEO + 2 * (f % 8)
+
+
+def estimate_slot(t):
+    e = t // 2
+    x, d = (3, 14) if e == PAIRS - 1 else (e // 7, 2 * (e % 7) + 1)
+    return (x * 2 + t % 2) * PER_GEO + d
+
+
+def sums_kernel(idx_hbm, wgt_hbm, est_hbm, fac_hbm, var_hbm, out,
+                idx, wgt, est, fac, var, in_sem,
                 pk, varp, table, weight, block, sums, coded,
-                ready, own_sem, pk_send, pk_recv, row_send, row_recv,
+                ready, own_sem, pk_send, pk_recv, row_send, row_recv, fwd_send, fwd_recv,
                 tile_send, slot_recv, right_send, left_send, core_send, core_recv):
     g = lax.axis_index("geo")
     d = lax.axis_index("dist")
     me = g * DIST + d
-    tau = g * PER_GEO + d
     mine = d < PER_GEO
     x, c = lax.div(g, 2), lax.rem(g, 2)
+    even = lax.rem(d, 2) == 0
+    my_pair = even_pair(x, d)
+    is_hi = jnp.logical_and(even, my_pair == HI)
+    is_lo = jnp.logical_and(even, my_pair == LO)
+    at_home = lax.div(d, HALF) == c
     g_right = lax.rem(x + 1, 4) * 2 + c
     g_left = lax.rem(x + 3, 4) * 2 + c
     g_far = lax.rem(x + 2, 4) * 2 + c
@@ -45,33 +73,50 @@
     for s in range(1, GEO):
         pl.semaphore_signal(barrier, inc=1, device_id=(lax.rem(g + s, GEO), d), device_id_type=MESH)
 
+    loads = [pltpu.make_async_copy(src, dst, in_sem.at[n]) for n, (src, dst) in enumerate(
+        ((idx_hbm, idx), (wgt_hbm, wgt), (var_hbm, var), (est_hbm, est), (fac_hbm, fac)))]
+    for load in loads:
+        load.start()
+
+    loads[0].wait()
+    loads[1].wait()
     pk[d] = idx[...] * 512 + wgt[...]
     varp[...] = jnp.zeros_like(varp)
+    loads[2].wait()
     varp[:, 0:AGES] = var[...]
+    loads[3].wait()
+    loads[4].wait()
 
     my_rows = table.at[pl.ds(pl.multiple_of(me * ROWS, 16), ROWS), :]
 
-    def row_copy(ge, de, src, cols):
+    def row_copy(xe, de, src, cols):
         return pltpu.make_async_remote_copy(
             src_ref=src.at[:, cols], dst_ref=my_rows, send_sem=row_send.at[0],
-            recv_sem=row_recv.at[g], device_id=(ge, de), device_id_type=MESH)
-
-    def for_tile(t, action):
-        @pl.when(t < TABLE_TILES)
-        def _():
-            action(est, pl.ds(pl.multiple_of(t * LANES, LANES), LANES))
-
-        @pl.when(jnp.logical_and(t >= TABLE_TILES, t < HI))
-        def _():
-            action(fac, pl.ds(pl.multiple_of((t - TABLE_TILES) * LANES, LANES), LANES))
-
-        @pl.when(t >= HI)
-        def _():
-            action(varp, pl.ds(0, LANES))
-
-    @pl.when(mine)
-    def _():
-        for_tile(tau, lambda src, cols: pltpu.make_async_copy(src.at[:, cols], my_rows, row_recv.at[g]).start())
+            recv_sem=row_recv.at[x], device_id=(xe * 2 + c, de), device_id_type=MESH)
+
+    def of_pair(src, pair):
+        return src, pl.ds(pl.multiple_of(pair * WIDE, WIDE), WIDE)
+
+    def for_even(f, also, action):
+        @pl.when(jnp.logical_and(also, f < PAIRS))
+        def _():
+            action(*of_pair(fac, f))
+
+        @pl.when(jnp.logical_and(also, jnp.logical_and(f >= PAIRS, f <= LO)))
+        def _():
+            action(varp, pl.ds(0, WIDE))
+
+        @pl.when(jnp.logical_and(also, f > LO))
+        def _():
+            action(*of_pair(est, PAIRS - 1))
+
+    def own_rows(src, cols):
+        pltpu.make_async_copy(src.at[:, cols], my_rows, row_recv.at[x]).start()
+    for_even(my_pair, even, own_rows)
+
+    @pl.when(jnp.logical_and(jnp.logical_not(even), mine))
+    def _():
+        own_rows(*of_pair(est, odd_pair(x, d)))
 
     pl.semaphore_wait(barrier, DIST - 1 + GEO - 1)
     for s in range(1, GEO):
@@ -82,34 +127,48 @@
             src_ref=pk.at[slot], dst_ref=pk.at[slot], send_sem=pk_send.at[0],
             recv_sem=pk_recv.at[0], device_id=(g, to), device_id_type=MESH)
 
-    def pk_start(s, _):
-        pk_copy(d, lax.rem(d + s, DIST)).start()
-        return 0
-    lax.fori_loop(1, DIST, pk_start, 0)
-
-    def rows_to(r, ks):
-        ge = lax.rem(g + r, GEO)
-
+    @pl.when(at_home)
+    def _():
+        def pk_start(s, _):
+            pk_copy(d, lax.rem(d + s, DIST)).start()
+            return 0
+        lax.fori_loop(1, DIST, pk_start, 0)
+
+    def rows_to(r):
         def one(k, _):
-            de = lax.rem(d + k, DIST)
-
-            @pl.when(de < PER_GEO)
-            def _():
-                for_tile(ge * PER_GEO + de, lambda src, cols: row_copy(ge, de, src, cols).start())
+            spot = lax.rem(lax.div(d, 2) + k, HALF)
+            de = 2 * spot
+            xe = lax.rem(x + r + de, 4)
+            other = jnp.logical_or(xe != x, de != d)
+            for_even(even_pair(xe, de), other, lambda src, cols: row_copy(xe, de, src, cols).start())
+            do = 2 * spot + 1
+            xo = lax.rem(x + r + do, 4)
+
+            @pl.when(jnp.logical_and(do < PER_GEO, jnp.logical_or(xo != x, do != d)))
+            def _():
+                row_copy(xo, do, *of_pair(est, odd_pair(xo, do))).start()
             return 0
-        lax.fori_loop(ks, DIST, one, 0)
-        return 0
-    rows_to(0, 1)
+        lax.fori_loop(0, HALF, one, 0)
     pl.semaphore_wait(ready, GEO - 1)
-    lax.fori_loop(1, GEO, lambda r, _: rows_to(r, 0), 0)
-
-    others = pk.at[pl.ds(0, DIST - 1)]
-    pltpu.make_async_copy(others, others, pk_recv.at[0]).wait()
+    for r in range(AHEAD):
+        rows_to(r)
+
+    def pk_wait(n, sem):
+        ref = pk.at[pl.ds(0, n)]
+        pltpu.make_async_copy(ref, ref, sem.at[0]).wait()
+
+    @pl.when(at_home)
+    def _():
+        pk_wait(HALF - 1, pk_recv)
+
+    @pl.when(jnp.logical_not(at_home))
+    def _():
+        pk_wait(HALF, pk_recv)
     lane = lax.broadcasted_iota(jnp.int32, (DB, LANES), 1)
     residue = lax.broadcasted_iota(jnp.int32, (64, DB), 0)
 
-    def weights_of(dd, _):
-        entries = pk[dd]
+    def weights_of(n, _):
+        entries = pk[c * HALF + n]
         res = lax.shift_right_logical(entries, 9) & 63
         val = (lax.shift_right_logical(entries, 15) * 512) + (entries & 511)
         acc = jnp.zeros((64, DB), jnp.int32)
@@ -118,13 +177,12 @@
         both = jnp.transpose(jnp.concatenate([acc, acc], axis=0))
         w = both & 511
         square = w * w
-        w = jnp.where(tau == HI, lax.shift_right_logical(square, 8),
-                      jnp.where(tau == LO, square & 255, w))
+        w = jnp.where(is_hi, lax.shift_right_logical(square, 8), jnp.where(is_lo, square & 255, w))
         b = lax.shift_right_logical(both, 9) - jnp.where(lane >= 64, 1, 0)
-        weight[dd] = (w.astype(jnp.float32) * (1.0 / 256.0)).astype(jnp.bfloat16)
-        block[dd] = b.astype(jnp.float32).astype(jnp.bfloat16)
+        weight[n] = (w.astype(jnp.float32) * (1.0 / 256.0)).astype(jnp.bfloat16)
+        block[n] = b.astype(jnp.float32).astype(jnp.bfloat16)
         return 0
-    lax.fori_loop(0, DIST, weights_of, 0)
+    lax.fori_loop(0, HALF, weights_of, 0)
 
     many = 4
 
@@ -141,59 +199,88 @@
             rows = table[pl.ds(pl.multiple_of(gb * BLOCK + step * 256, 256), 256), :]
             part = jnp.dot(jnp.concatenate(parts, axis=1), rows, preferred_element_type=jnp.float32)
             total = part if total is None else total + part
-        return total.reshape(many, DB, LANES)
-
-    def tile_copy(dd):
+        return total.reshape(many, DB, WIDE)
+
+    def tile_copy(n, h):
+        slot = (x * 2 + h) * PER_GEO + d
         return pltpu.make_async_remote_copy(
-            src_ref=coded.at[dd], dst_ref=out.at[tau], send_sem=tile_send.at[0],
-            recv_sem=slot_recv.at[tau], device_id=(g, dd), device_id_type=MESH)
+            src_ref=coded.at[n, h], dst_ref=out.at[slot], send_sem=tile_send.at[0],
+            recv_sem=slot_recv.at[slot], device_id=(x * 2 + h, c * HALF + n), device_id_type=MESH)
 
     def own_tile_copy():
-        return pltpu.make_async_copy(coded.at[d], out.at[tau], own_sem)
-
-    def encode(dd):
-        total = sums[dd]
-        top = jnp.maximum(jnp.max(jnp.abs(total), axis=0, keepdims=True), 1e-30)
-        e = jnp.ceil(jnp.log2(top))
-        code = jnp.round(total * (STEPS / jnp.exp2(e)))
-        coded[dd, 0:DB, :] = code.astype(jnp.int32).astype(jnp.int16)
-        coded[dd, DB:CODE_ROWS, :] = jnp.broadcast_to(e, (8, LANES)).astype(jnp.int32).astype(jnp.int16)
-
-    @pl.when(mine)
-    def _():
-        def block_of(r, _):
-            gb = lax.rem(g + GEO - r, GEO)
-            rows = table.at[pl.ds(pl.multiple_of(gb * BLOCK, 256), BLOCK), :]
-            pltpu.make_async_copy(rows, rows, row_recv.at[gb]).wait()
-
-            def quarter(i, _):
-                q = lax.rem(lax.div(d, many) + i, DIST // many)
-
-                @pl.when(r == 0)
-                def _():
-                    sums[pl.ds(q * many, many)] = product(q, gb)
-
-                @pl.when(r > 0)
-                def _():
-                    sums[pl.ds(q * many, many)] += product(q, gb)
-
-                @pl.when(r == GEO - 1)
-                def _():
-                    for k in range(many):
-                        dd = q * many + lax.rem(lax.rem(d, many) + k, many)
-                        encode(dd)
-
-                        @pl.when(dd != d)
+        return pltpu.make_async_copy(coded.at[d - c * HALF, c], out.at[g * PER_GEO + d], own_sem)
+
+    def encode(n):
+        for h in range(2):
+            total = sums[n, :, h * LANES:(h + 1) * LANES]
+            top = jnp.maximum(jnp.max(jnp.abs(total), axis=0, keepdims=True), 1e-30)
+            e = jnp.ceil(jnp.log2(top))
+            code = jnp.round(total * (STEPS / jnp.exp2(e)))
+            coded[n, h, 0:DB, :] = code.astype(jnp.int32).astype(jnp.int16)
+            coded[n, h, DB:CODE_ROWS, :] = jnp.broadcast_to(e, (8, LANES)).astype(jnp.int32).astype(jnp.int16)
+
+    first = lax.rem(lax.div(d, many), 2)
+
+    def add_block(gb, start, finish):
+        def part(i, _):
+            q = lax.rem(first + i, 2)
+
+            @pl.when(start)
+            def _():
+                sums[pl.ds(q * many, many)] = product(q, gb)
+
+            @pl.when(jnp.logical_not(start))
+            def _():
+                sums[pl.ds(q * many, many)] += product(q, gb)
+
+            @pl.when(finish)
+            def _():
+                for k in range(many):
+                    n = q * many + lax.rem(lax.rem(d, many) + k, many)
+                    encode(n)
+                    for h in range(2):
+                        own = jnp.logical_and(c * HALF + n == d, c == h)
+
+                        @pl.when(jnp.logical_not(own))
                         def _():
-                            tile_copy(dd).start()
-
-                        @pl.when(dd == d)
+                            tile_copy(n, h).start()
+
+                        @pl.when(own)
                         def _():
                             own_tile_copy().start()
-                return 0
-            lax.fori_loop(0, DIST // many, quarter, 0)
             return 0
-        lax.fori_loop(0, GEO, block_of, 0)
+        lax.fori_loop(0, 2, part, 0)
+
+    def block_at(gb):
+        return table.at[pl.ds(pl.multiple_of(gb * BLOCK, 256), BLOCK), :]
+
+    def pass_on(xs):
+        rows = block_at(xs * 2 + c)
+        return pltpu.make_async_remote_copy(
+            src_ref=rows, dst_ref=rows, send_sem=fwd_send.at[0], recv_sem=fwd_recv.at[xs],
+            device_id=(g_core, d), device_id_type=MESH)
+
+    def block_of(r, _):
+        xs = lax.rem(x + 8 - lax.rem(d, 4) - r, 4)
+
+        @pl.when(mine)
+        def _():
+            rows = block_at(xs * 2 + c)
+            pltpu.make_async_copy(rows, rows, row_recv.at[xs]).wait()
+            pass_on(xs).start()
+
+        @pl.when(r < 4 - AHEAD)
+        def _():
+            rows_to(r + AHEAD)
+
+        @pl.when(mine)
+        def _():
+            add_block(xs * 2 + c, r == 0, r < 0)
+            rows = block_at(xs * 2 + 1 - c)
+            pltpu.make_async_copy(rows, rows, fwd_recv.at[xs]).wait()
+            add_block(xs * 2 + 1 - c, r < 0, r == 3)
+        return 0
+    lax.fori_loop(0, 4, block_of, 0)
 
     def slot_copy(slot, send_sem, recv_sem, to_g):
         return pltpu.make_async_remote_copy(
@@ -207,9 +294,10 @@
         slot_copy(slot, core_send.at[0], core_recv.at[0], g_core).start()
 
     def source(j):
-        i, k = lax.div(j, many), lax.rem(j, many)
-        return (lax.rem(lax.div(d, many) + DIST // many - i, DIST // many) * many
-                + lax.rem(lax.rem(d, many) + many - k, many))
+        odd = lax.div(j, 8)
+        i, m, b = lax.rem(lax.div(j, 4), 2), lax.rem(lax.div(j, 2), 2), lax.rem(j, 2)
+        k = 2 * m + lax.rem(d + odd, 2)
+        return b * HALF + lax.rem(first + i, 2) * many + lax.rem(lax.rem(d, many) + many - k, many)
 
     def from_dist(j):
         dd = source(j)
@@ -217,11 +305,13 @@
 
         @pl.when(dd < PER_GEO)
         def _():
-            @pl.when(dd == d)
+            own = jnp.logical_and(dd == d, at_home)
+
+            @pl.when(own)
             def _():
                 own_tile_copy().wait()
 
-            @pl.when(dd != d)
+            @pl.when(jnp.logical_not(own))
             def _():
                 arrived(slot)
             slot_copy(slot, right_send.at[0], slot_recv.at[slot], g_right).start()
@@ -236,13 +326,13 @@
         def _():
             arrived(from_left)
 
-            @pl.when(lax.rem(dd, 2) == 0)
+            @pl.when(lax.rem(lax.div(dd, 2), 2) == 0)
             def _():
                 slot_copy(from_left, right_send.at[1], slot_recv.at[from_left], g_right).start()
             to_core(from_left)
             arrived(from_right)
 
-            @pl.when(lax.rem(dd, 2) == 1)
+            @pl.when(lax.rem(lax.div(dd, 2), 2) == 1)
             def _():
                 slot_copy(from_right, left_send.at[1], slot_recv.at[from_right], g_left).start()
             to_core(from_right)
@@ -278,18 +368,31 @@
     wait_slots(left_send.at[0], PER_GEO)
     wait_slots(right_send.at[1], 8)
     wait_slots(left_send.at[1], 7)
-    pltpu.make_async_copy(others, others, pk_send.at[0]).wait()
+
+    @pl.when(at_home)
+    def _():
+        pk_wait(DIST - 1, pk_send)
+
+    def wait_rows(sem, n):
+        ref = table.at[pl.ds(0, n), :]
+        pltpu.make_async_copy(ref, ref, sem.at[0]).wait()
 
     @pl.when(mine)
     def _():
-        wait_slots(tile_send.at[0], DIST - 1)
-        ref = table.at[pl.ds(0, (SLOTS - 1) * ROWS), :]
-        pltpu.make_async_copy(ref, ref, row_send.at[0]).wait()
+        wait_rows(row_send, (4 * PER_GEO - 1) * ROWS)
+        wait_rows(fwd_send, 4 * BLOCK)
+
+        @pl.when(at_home)
+        def _():
+            wait_slots(tile_send.at[0], DIST - 1)
+
+        @pl.when(jnp.logical_not(at_home))
+        def _():
+            wait_slots(tile_send.at[0], DIST)
 
     @pl.when(jnp.logical_not(mine))
     def _():
-        ref = table.at[pl.ds(0, SLOTS * ROWS), :]
-        pltpu.make_async_copy(ref, ref, row_send.at[0]).wait()
+        wait_rows(row_send, 4 * PER_GEO * ROWS)
 
 
 def tile_sums(idx, wgt, est, fac, var):
@@ -299,17 +402,23 @@
     return pl.pallas_call(
         sums_kernel,
         out_shape=jax.ShapeDtypeStruct((SLOTS, CODE_ROWS, LANES), jnp.int16),
-        in_specs=[vmem, vmem, hbm, hbm, vmem],
+        in_specs=[hbm] * 5,
         out_specs=vmem,
         scratch_shapes=[
+            pltpu.VMEM((INTER, DB), jnp.int32),
+            pltpu.VMEM((INTER, DB), jnp.int32),
+            pltpu.VMEM(est.shape, jnp.bfloat16),
+            pltpu.VMEM(fac.shape, jnp.bfloat16),
+            pltpu.VMEM(var.shape, jnp.bfloat16),
+            dma((5,)),
             pltpu.VMEM((DIST, INTER, DB), jnp.int32),
-            pltpu.VMEM((ROWS, LANES), jnp.bfloat16),
-            pltpu.VMEM((TRACTS, LANES), jnp.bfloat16),
-            pltpu.VMEM((DIST, DB, LANES), jnp.bfloat16),
-            pltpu.VMEM((DIST, DB, LANES), jnp.bfloat16),
-            pltpu.VMEM((DIST, DB, LANES), jnp.float32),
-            pltpu.VMEM((DIST, CODE_ROWS, LANES), jnp.int16),
-            pltpu.SemaphoreType.REGULAR, dma(()), dma((1,)), dma((1,)), dma((1,)), dma((GEO,)),
+            pltpu.VMEM((ROWS, WIDE), jnp.bfloat16),
+            pltpu.VMEM((TRACTS, WIDE), jnp.bfloat16),
+            pltpu.VMEM((HALF, DB, LANES), jnp.bfloat16),
+            pltpu.VMEM((HALF, DB, LANES), jnp.bfloat16),
+            pltpu.VMEM((HALF, DB, WIDE), jnp.float32),
+            pltpu.VMEM((HALF, 2, CODE_ROWS, LANES), jnp.int16),
+            pltpu.SemaphoreType.REGULAR, dma(()), dma((1,)), dma((1,)), dma((1,)), dma((4,)), dma((1,)), dma((4,)),
             dma((1,)), dma((SLOTS,)), dma((2,)), dma((2,)), dma((1,)), dma((1,)),
         ],
         compiler_params=pltpu.CompilerParams(has_side_effects=True, collective_id=0, vmem_limit_bytes=40 * 2**20),
@@ -329,16 +438,14 @@
         return code * (jnp.exp2(e[0:1, :]) * (1.0 / STEPS))
 
     for t in range(TABLE_TILES):
-        marg[:, t * LANES:(t + 1) * LANES] = decode(t)
+        marg[:, t * LANES:(t + 1) * LANES] = decode(estimate_slot(t))
     out_marg = pltpu.make_async_copy(marg, marg_hbm, marg_sem)
     out_marg.start()
 
-    noise[...] = jnp.transpose(decode(HI) + decode(LO) * (1.0 / 256.0))
-
-    def load_tile(t, _):
-        loading[pl.ds(pl.multiple_of(t * DB, DB), DB), :] = decode(TABLE_TILES + t)
-        return 0
-    lax.fori_loop(0, TABLE_TILES, load_tile, 0)
+    noise[...] = jnp.transpose(decode(factor_slot(2 * HI)) + decode(factor_slot(2 * LO)) * (1.0 / 256.0))
+
+    for t in range(TABLE_TILES):
+        loading[t * DB:(t + 1) * DB, :] = decode(factor_slot(t))
 
     paired[...] = jnp.zeros_like(paired)
     lane_row = lax.broadcasted_iota(jnp.int32, (TABLE_TILES, LANES), 1)
@@ -412,7 +519,8 @@
 
 
 def shards(estimates, factors, variances, intersection_tracts, intersection_weights):
-    slots = tile_sums(intersection_tracts.T, intersection_weights.T, estimates, factors, variances)
+    keep = lambda a: pltpu.with_memory_space_constraint(a, pltpu.MemorySpace.HBM)
+    slots = tile_sums(keep(intersection_tracts.T), keep(intersection_weights.T), keep(estimates), keep(factors), keep(variances))
     return blocks(slots)
 
 

time: 86.7 us -> 77.8 us (0.90)
  Pallas kernels: 81.4 us -> 77 us
  local copies, waits for them, and re-layouts: 4.35 us -> 0 us
    unnamed x10 -> x0, local copies, waits for them, and re-layouts: 4.35 us -> none
    pallas_call x1, Pallas kernels: 68.2 us -> 64.5 us  [tile_sums(): pl.pallas_call(sums_kernel, out_shape=jax.ShapeDtypeStruct((SLOTS, CODE_R...]
where the time goes in v3:
time: 77.8 us; the launch traced here: 77.7 us
  Pallas kernels  77 us (99%)
    pallas_call x1, Pallas kernels, tile_sums(): pl.pallas_call(sums_kernel, out_shape=jax.ShapeDtypeStruct((SLOTS, CODE_R...  64.5 us
    pallas_call x1, Pallas kernels, blocks(): pl.pallas_call(blocks_kernel, out_shape=(jax.ShapeDtypeStruct((DB, TABLE_...  12.5 us

profile of v3, /device:TPU:1, one launch (start us, length us, event | category | flops | bytes accessed | tf_op | source)
XLA Modules:
  0.0 77.7 jit_solution(6218365986531896874)
XLA Ops:
  0.6 64.5 %tile_sums.1.slots = s16[120,136,128]{2,1,0:T(8,128)(2,1)S(1)} custom-call(s32[32,128]{1,0:T(8,128)} %bitcast.3, s32[32,128]{1,0:T(8,128)} %bitcast.4, bf16[48,7424]{1,0:T(8,128)(2,1)} %est_hbm.1, bf16[48,7424]{1,0:T(8,128)(2,1)} %fac_hbm.1, bf16[48,116]{1,0:T(8,128)(2,1)} %var_hbm.1), custom_call_target="tpu_custom_call" | custom-call | tf_op jit(solution)/shard_map/tile_sums/pallas_call | solution.py:402
  65.1 12.5 %district_blocks.1 = (f32[128,7424]{1,0:T(8,128)}, f32[13456,128]{1,0:T(8,128)}) custom-call(s16[120,136,128]{2,1,0:T(8,128)(2,1)S(1)} %tile_sums.1.slots), custom_call_target="tpu_custom_call" | custom-call | tf_op jit(solution)/shard_map/district_blocks/pallas_call | solution.py:500

commit v4 on v3

v4 whole, which is shorter than its diff:
```python
import jax
import jax.numpy as jnp
from jax import lax
from jax.experimental import pallas as pl
from jax.experimental.pallas import tpu as pltpu
from jax.sharding import PartitionSpec as P

MESH = pl.DeviceIdType.MESH
GEO, DIST = 8, 16
DEVICES = GEO * DIST
LANES = 128
ROWS = 48
TRACTS = ROWS * DEVICES
BLOCK = ROWS * DIST
DB = 128
INTER = 32
TABLE_TILES = 58
HI, LO = TABLE_TILES, TABLE_TILES + 1
PER_X = 15
CHIPS = 4 * PER_X
HALF = DIST // 2
SLOTS = 2 * CHIPS
CODE_ROWS = DB + 8
STEPS = 32000.0
AGES, RANK = 116, 64
AHEAD = 3


def sums_kernel(idx_hbm, wgt_hbm, est_hbm, fac_hbm, var_hbm, out,
                idx, wgt, est, fac, var, in_sem,
                pk, varp, table, weight, block, sums, coded,
                ready, own_sem, pk_send, pk_recv, row_send, row_recv, fwd_send, fwd_recv,
                tile_send, slot_recv, right_send, left_send, core_send, core_recv):
    g = lax.axis_index("geo")
    d = lax.axis_index("dist")
    me = g * DIST + d
    mine = d < PER_X
    x, c = lax.div(g, 2), lax.rem(g, 2)
    my_tile = x * PER_X + d
    at_home = lax.div(d, HALF) == c
    g_right = lax.rem(x + 1, 4) * 2 + c
    g_left = lax.rem(x + 3, 4) * 2 + c
    g_far = lax.rem(x + 2, 4) * 2 + c
    g_core = x * 2 + (1 - c)

    barrier = pltpu.get_barrier_semaphore()
    for s in range(1, DIST):
        pl.semaphore_signal(barrier, inc=1, device_id=(g, lax.rem(d + s, DIST)), device_id_type=MESH)
    for s in range(1, GEO):
        pl.semaphore_signal(barrier, inc=1, device_id=(lax.rem(g + s, GEO), d), device_id_type=MESH)

    loads = [pltpu.make_async_copy(src, dst, in_sem.at[n]) for n, (src, dst) in enumerate(
        ((idx_hbm, idx), (wgt_hbm, wgt), (var_hbm, var), (est_hbm, est), (fac_hbm, fac)))]
    for load in loads:
        load.start()

    loads[0].wait()
    loads[1].wait()
    pk[d] = idx[...] * 512 + wgt[...]
    varp[...] = jnp.zeros_like(varp)
    loads[2].wait()
    varp[:, 0:AGES] = var[...]
    loads[3].wait()
    loads[4].wait()

    my_range = pl.ds(pl.multiple_of(me * ROWS, 16), ROWS)
    sources = (fac, est)

    def for_tile(kind, t, also, action):
        @pl.when(jnp.logical_and(also, t < TABLE_TILES))
        def _():
            action(sources[kind].at[:, pl.ds(pl.multiple_of(t * LANES, LANES), LANES)])

        @pl.when(jnp.logical_and(also, t >= TABLE_TILES))
        def _():
            action(varp)

    for kind in range(2):
        for_tile(kind, my_tile, mine, lambda src: pltpu.make_async_copy(
            src, table.at[kind, my_range, :], row_recv.at[kind * 4 + x]).start())

    pl.semaphore_wait(barrier, DIST - 1 + GEO - 1)
    for s in range(1, GEO):
        pl.semaphore_signal(ready, inc=1, device_id=(lax.rem(g + s, GEO), d), device_id_type=MESH)

    def pk_copy(slot, to):
        return pltpu.make_async_remote_copy(
            src_ref=pk.at[slot], dst_ref=pk.at[slot], send_sem=pk_send.at[0],
            recv_sem=pk_recv.at[0], device_id=(g, to), device_id_type=MESH)

    @pl.when(at_home)
    def _():
        def pk_start(s, _):
            pk_copy(d, lax.rem(d + s, DIST)).start()
            return 0
        lax.fori_loop(1, DIST, pk_start, 0)

    def rows_to(kind, r):
        def one(k, _):
            de = lax.rem(d + k, DIST)
            xe = lax.rem(x + r + de, 4)
            other = jnp.logical_and(de < PER_X, jnp.logical_or(xe != x, de != d))
            for_tile(kind, xe * PER_X + de, other, lambda src: pltpu.make_async_remote_copy(
                src_ref=src, dst_ref=table.at[kind, my_range, :], send_sem=row_send.at[kind],
                recv_sem=row_recv.at[kind * 4 + x], device_id=(xe * 2 + c, de), device_id_type=MESH).start())
            return 0
        lax.fori_loop(0, DIST, one, 0)
    pl.semaphore_wait(ready, GEO - 1)
    for r in range(AHEAD):
        rows_to(0, r)

    def pk_wait(n, sem):
        ref = pk.at[pl.ds(0, n)]
        pltpu.make_async_copy(ref, ref, sem.at[0]).wait()

    @pl.when(at_home)
    def _():
        pk_wait(HALF - 1, pk_recv)

    @pl.when(jnp.logical_not(at_home))
    def _():
        pk_wait(HALF, pk_recv)
    lane = lax.broadcasted_iota(jnp.int32, (DB, LANES), 1)
    residue = lax.broadcasted_iota(jnp.int32, (64, DB), 0)

    def weights_of(n, _):
        entries = pk[c * HALF + n]
        res = lax.shift_right_logical(entries, 9) & 63
        val = (lax.shift_right_logical(entries, 15) * 512) + (entries & 511)
        acc = jnp.zeros((64, DB), jnp.int32)
        for k in range(INTER):
            acc = jnp.where(residue == res[k:k + 1, :], val[k:k + 1, :], acc)
        both = jnp.transpose(jnp.concatenate([acc, acc], axis=0))
        w = both & 511
        square = w * w
        w = jnp.where(my_tile == HI, lax.shift_right_logical(square, 8), jnp.where(my_tile == LO, square & 255, w))
        b = lax.shift_right_logical(both, 9) - jnp.where(lane >= 64, 1, 0)
        weight[n] = (w.astype(jnp.float32) * (1.0 / 256.0)).astype(jnp.bfloat16)
        block[n] = b.astype(jnp.float32).astype(jnp.bfloat16)
        return 0
    lax.fori_loop(0, HALF, weights_of, 0)

    many = 4

    def add_block(kind, gb):
        def part(q, _):
            w = weight[pl.ds(q * many, many)].reshape(many * DB, LANES)
            b = block[pl.ds(q * many, many)].reshape(many * DB, LANES)
            zero = jnp.zeros_like(w)
            total = None
            for step in range(BLOCK // 256):
                parts = []
                for h in range(2):
                    at = (2 * (gb * (BLOCK // LANES) + 2 * step + h)).astype(jnp.float32).astype(jnp.bfloat16)
                    parts.append(jnp.where(b == at, w, zero))
                rows = table[kind, pl.ds(pl.multiple_of(gb * BLOCK + step * 256, 256), 256), :]
                product = jnp.dot(jnp.concatenate(parts, axis=1), rows, preferred_element_type=jnp.float32)
                total = product if total is None else total + product
            sums[pl.ds(q * many, many)] += total.reshape(many, DB, LANES)
            return 0
        lax.fori_loop(0, HALF // many, part, 0)

    def block_rows(kind, gb):
        return table.at[kind, pl.ds(pl.multiple_of(gb * BLOCK, 256), BLOCK), :]

    def phase(kind, r, then):
        xs = lax.rem(x + 8 - lax.rem(d, 4) - r, 4)
        n = kind * 4 + xs
        own, other = xs * 2 + c, xs * 2 + 1 - c

        @pl.when(mine)
        def _():
            rows = block_rows(kind, own)
            pltpu.make_async_copy(rows, rows, row_recv.at[n]).wait()
            pltpu.make_async_remote_copy(
                src_ref=rows, dst_ref=rows, send_sem=fwd_send.at[kind], recv_sem=fwd_recv.at[n],
                device_id=(g_core, d), device_id_type=MESH).start()
        then()

        @pl.when(mine)
        def _():
            add_block(kind, own)
            rows = block_rows(kind, other)
            pltpu.make_async_copy(rows, rows, fwd_recv.at[n]).wait()
            add_block(kind, other)

    def side_of(kind, dd):
        return lax.rem(dd + kind, 2)

    def tile_copy(kind, n):
        slot = kind * CHIPS + my_tile
        return pltpu.make_async_remote_copy(
            src_ref=coded.at[kind, n], dst_ref=out.at[slot], send_sem=tile_send.at[kind], recv_sem=slot_recv.at[slot],
            device_id=(x * 2 + side_of(kind, d), c * HALF + n), device_id_type=MESH)

    def own_tile_copy(kind):
        return pltpu.make_async_copy(coded.at[kind, d - c * HALF], out.at[kind * CHIPS + my_tile], own_sem.at[kind])

    def stays(kind, dd):
        return jnp.logical_and(jnp.logical_and(dd == d, at_home), side_of(kind, d) == c)

    first = lax.rem(lax.div(d, many), 2)

    def encode(kind):
        def one(i, _):
            n = lax.rem(first + lax.div(i, many), 2) * many + lax.rem(d + i, many)
            total = sums[n]
            top = jnp.maximum(jnp.max(jnp.abs(total), axis=0, keepdims=True), 1e-30)
            e = jnp.ceil(jnp.log2(top))
            code = jnp.round(total * (STEPS / jnp.exp2(e)))
            coded[kind, n, 0:DB, :] = code.astype(jnp.int32).astype(jnp.int16)
            coded[kind, n, DB:CODE_ROWS, :] = jnp.broadcast_to(e, (8, LANES)).astype(jnp.int32).astype(jnp.int16)
            own = stays(kind, c * HALF + n)

            @pl.when(jnp.logical_not(own))
            def _():
                tile_copy(kind, n).start()

            @pl.when(own)
            def _():
                own_tile_copy(kind).start()
            return 0
        lax.fori_loop(0, HALF, one, 0)
        sums[...] = jnp.zeros_like(sums)

    def slot_copy(slot, send_sem, recv_sem, to_g):
        return pltpu.make_async_remote_copy(
            src_ref=out.at[slot], dst_ref=out.at[slot], send_sem=send_sem,
            recv_sem=recv_sem, device_id=(to_g, d), device_id_type=MESH)

    def arrived(slot):
        pltpu.make_async_copy(out.at[slot], out.at[slot], slot_recv.at[slot]).wait()

    def to_core(kind, slot):
        slot_copy(slot, core_send.at[0], core_recv.at[kind], g_core).start()

    def source(kind, j):
        i, m, b = lax.div(j, 4), lax.rem(lax.div(j, 2), 2), lax.rem(j, 2)
        k = 2 * m + lax.rem(d + c + kind, 2)
        return b * HALF + lax.rem(first + i, 2) * many + lax.rem(lax.rem(d, many) + many - k, many)

    def slot_at(kind, xx, dd):
        return kind * CHIPS + xx * PER_X + dd

    def from_dist(kind, j):
        dd = source(kind, j)
        slot = slot_at(kind, x, dd)

        @pl.when(dd < PER_X)
        def _():
            own = stays(kind, dd)

            @pl.when(own)
            def _():
                own_tile_copy(kind).wait()

            @pl.when(jnp.logical_not(own))
            def _():
                arrived(slot)
            slot_copy(slot, right_send.at[0], slot_recv.at[slot], g_right).start()
            slot_copy(slot, left_send.at[0], slot_recv.at[slot], g_left).start()
            to_core(kind, slot)

    def from_sides(kind, j):
        dd = source(kind, j)
        from_left = slot_at(kind, lax.rem(x + 3, 4), dd)
        from_right = slot_at(kind, lax.rem(x + 1, 4), dd)

        @pl.when(dd < PER_X)
        def _():
            arrived(from_left)

            @pl.when(lax.rem(lax.div(dd, 2), 2) == 0)
            def _():
                slot_copy(from_left, right_send.at[1], slot_recv.at[from_left], g_right).start()
            to_core(kind, from_left)
            arrived(from_right)

            @pl.when(lax.rem(lax.div(dd, 2), 2) == 1)
            def _():
                slot_copy(from_right, left_send.at[1], slot_recv.at[from_right], g_left).start()
            to_core(kind, from_right)

    def from_far(kind, j):
        dd = source(kind, j)

        @pl.when(dd < PER_X)
        def _():
            slot = slot_at(kind, lax.rem(x + 2, 4), dd)
            arrived(slot)
            to_core(kind, slot)

    def many_of(body, kind, start, stop):
        def one(j, _):
            body(kind, j)
            return 0
        lax.fori_loop(start, stop, one, 0)

    sums[...] = jnp.zeros_like(sums)
    for n in range(8):
        kind, r = n // 4, n % 4

        def then():
            if n + AHEAD < 8:
                rows_to((n + AHEAD) // 4, (n + AHEAD) % 4)
        phase(kind, r, then)
        if r == 3:
            @pl.when(mine)
            def _():
                encode(kind)
        if n == 5:
            many_of(from_dist, 0, 0, 4)
        if n == 6:
            many_of(from_dist, 0, 4, 8)
    many_of(from_sides, 0, 0, 8)
    many_of(from_dist, 1, 0, 8)
    many_of(from_far, 0, 0, 8)
    many_of(from_sides, 1, 0, 8)
    many_of(from_far, 1, 0, 8)

    def wait_slots(sem, n):
        ref = out.at[pl.ds(0, n)]
        pltpu.make_async_copy(ref, ref, sem).wait()
    odd_side = jnp.where(c == 1, 1, 0)
    for kind in range(2):
        @pl.when(odd_side == 1 - kind)
        def _():
            wait_slots(core_recv.at[kind], 4 * 8)

        @pl.when(odd_side == kind)
        def _():
            wait_slots(core_recv.at[kind], 4 * 7)
    wait_slots(core_send.at[0], 4 * PER_X)
    wait_slots(right_send.at[0], PER_X)
    wait_slots(left_send.at[0], PER_X)
    wait_slots(right_send.at[1], 8)
    wait_slots(left_send.at[1], 7)

    @pl.when(at_home)
    def _():
        pk_wait(DIST - 1, pk_send)

    for kind in range(2):
        def wait_rows(sem, n):
            ref = table.at[kind, pl.ds(0, n), :]
            pltpu.make_async_copy(ref, ref, sem.at[kind]).wait()

        @pl.when(mine)
        def _():
            wait_rows(row_send, (CHIPS - 1) * ROWS)
            wait_rows(fwd_send, 4 * BLOCK)
            own = stays(kind, d)

            @pl.when(own)
            def _():
                wait_slots(tile_send.at[kind], HALF - 1)

            @pl.when(jnp.logical_not(own))
            def _():
                wait_slots(tile_send.at[kind], HALF)

        @pl.when(jnp.logical_not(mine))
        def _():
            wait_rows(row_send, CHIPS * ROWS)


def tile_sums(idx, wgt, est, fac, var):
    vmem = pl.BlockSpec(memory_space=pltpu.VMEM)
    hbm = pl.BlockSpec(memory_space=pltpu.MemorySpace.HBM)
    dma = pltpu.SemaphoreType.DMA
    return pl.pallas_call(
        sums_kernel,
        out_shape=jax.ShapeDtypeStruct((SLOTS, CODE_ROWS, LANES), jnp.int16),
        in_specs=[hbm] * 5,
        out_specs=vmem,
        scratch_shapes=[
            pltpu.VMEM((INTER, DB), jnp.int32),
            pltpu.VMEM((INTER, DB), jnp.int32),
            pltpu.VMEM(est.shape, jnp.bfloat16),
            pltpu.VMEM(fac.shape, jnp.bfloat16),
            pltpu.VMEM(var.shape, jnp.bfloat16),
            dma((5,)),
            pltpu.VMEM((DIST, INTER, DB), jnp.int32),
            pltpu.VMEM((ROWS, LANES), jnp.bfloat16),
            pltpu.VMEM((2, TRACTS, LANES), jnp.bfloat16),
            pltpu.VMEM((HALF, DB, LANES), jnp.bfloat16),
            pltpu.VMEM((HALF, DB, LANES), jnp.bfloat16),
            pltpu.VMEM((HALF, DB, LANES), jnp.float32),
            pltpu.VMEM((2, HALF, CODE_ROWS, LANES), jnp.int16),
            pltpu.SemaphoreType.REGULAR, dma((2,)), dma((1,)), dma((1,)), dma((2,)), dma((8,)), dma((2,)), dma((8,)),
            dma((2,)), dma((SLOTS,)), dma((2,)), dma((2,)), dma((1,)), dma((2,)),
        ],
        compiler_params=pltpu.CompilerParams(has_side_effects=True, collective_id=0, vmem_limit_bytes=40 * 2**20),
        name="tile_sums",
    )(idx, wgt, est, fac, var)


GROUP = 8
CROWS = 120
CHUNK = 4


def blocks_kernel(slots, marg_hbm, cov_hbm, loading, marg, noise, paired, outer, flat, marg_sem, cov_sem):
    def decode(slot):
        code = slots[slot, 0:DB, :].astype(jnp.int32).astype(jnp.float32)
        e = slots[slot, DB:CODE_ROWS, :].astype(jnp.int32).astype(jnp.float32)
        return code * (jnp.exp2(e[0:1, :]) * (1.0 / STEPS))

    for t in range(TABLE_TILES):
        marg[:, t * LANES:(t + 1) * LANES] = decode(CHIPS + t)
    out_marg = pltpu.make_async_copy(marg, marg_hbm, marg_sem)
    out_marg.start()

    noise[...] = jnp.transpose(decode(HI) + decode(LO) * (1.0 / 256.0))

    for t in range(TABLE_TILES):
        loading[t * DB:(t + 1) * DB, :] = decode(t)

    paired[...] = jnp.zeros_like(paired)
    lane_row = lax.broadcasted_iota(jnp.int32, (TABLE_TILES, LANES), 1)
    lane_full = lax.broadcasted_iota(jnp.int32, (LANES, LANES), 1)
    sub = lax.broadcasted_iota(jnp.int32, (LANES, LANES), 0)

    def group(grp, _):
        for k in range(GROUP):
            rows = loading[pl.ds(grp * GROUP + k, TABLE_TILES, stride=DB), :]
            turned = pltpu.roll(rows, RANK, axis=1)
            low = lane_row < RANK
            paired[k, pl.ds(0, TABLE_TILES, stride=2), :] = jnp.where(low, rows, turned)
            paired[k, pl.ds(1, TABLE_TILES, stride=2), :] = jnp.where(low, turned, rows)
        for k in range(GROUP):
            full = paired[k]
            hi = full.astype(jnp.bfloat16)
            lo = (full - hi.astype(jnp.float32)).astype(jnp.bfloat16)
            mixed = jnp.where(lane_full < RANK, hi, lo)
            left = jnp.concatenate([mixed, mixed], axis=1)
            right = jnp.concatenate([hi, lo], axis=1)
            product = lax.dot_general(left, right, (((1,), (1,)), ((), ())), preferred_element_type=jnp.float32)
            outer[pl.ds(pl.multiple_of((grp * GROUP + k) * CROWS, 8), CROWS), :] = product[0:CROWS, :]
        return 0
    lax.fori_loop(0, DB // GROUP, group, 0)

    span = CHUNK * AGES

    def cov_copy(n):
        rows = pl.ds(pl.multiple_of(n * span, 8), span)
        return pltpu.make_async_copy(flat.at[rows, :], cov_hbm.at[rows, :], cov_sem)

    def ages(n, _):
        for pair in range(CHUNK // 2):
            halves = []
            for h in range(2):
                i = n * CHUNK + pair * 2 + h
                block = jnp.transpose(outer[pl.ds(i, DB, stride=CROWS), :])
                block = block + jnp.where(sub == i, noise[pl.ds(i, 1), :], 0.0)
                halves.append(block[0:AGES, :])
            flat[pl.ds(pl.multiple_of(n * span + pair * 2 * AGES, 8), 2 * AGES), :] = jnp.concatenate(halves, axis=0)
        cov_copy(n).start()
        return 0
    lax.fori_loop(0, AGES // CHUNK, ages, 0)
    pltpu.make_async_copy(flat, cov_hbm, cov_sem).wait()
    out_marg.wait()


def blocks(slots):
    vmem = pl.BlockSpec(memory_space=pltpu.VMEM)
    hbm = pl.BlockSpec(memory_space=pltpu.MemorySpace.HBM)
    dma = pltpu.SemaphoreType.DMA
    marg, cov = pl.pallas_call(
        blocks_kernel,
        out_shape=(jax.ShapeDtypeStruct((DB, TABLE_TILES * LANES), jnp.float32),
                   jax.ShapeDtypeStruct((AGES * AGES, DB), jnp.float32)),
        in_specs=[vmem],
        out_specs=(hbm, hbm),
        scratch_shapes=[
            pltpu.VMEM((TABLE_TILES * DB, LANES), jnp.float32),
            pltpu.VMEM((DB, TABLE_TILES * LANES), jnp.float32),
            pltpu.VMEM((DB, LANES), jnp.float32),
            pltpu.VMEM((GROUP, LANES, LANES), jnp.float32),
            pltpu.VMEM((DB * CROWS, LANES), jnp.float32),
            pltpu.VMEM((AGES * AGES, DB), jnp.float32),
            dma(()), dma(()),
        ],
        compiler_params=pltpu.CompilerParams(vmem_limit_bytes=48 * 2**20),
        name="district_blocks",
    )(slots)
    return marg, cov.T


def shards(estimates, factors, variances, intersection_tracts, intersection_weights):
    keep = lambda a: pltpu.with_memory_space_constraint(a, pltpu.MemorySpace.HBM)
    slots = tile_sums(keep(intersection_tracts.T), keep(intersection_weights.T), keep(estimates), keep(factors), keep(variances))
    return blocks(slots)


def solution(mesh):
    return jax.shard_map(
        shards,
        mesh=mesh,
        in_specs=(
            P(("geo", "dist"), None),
            P(("geo", "dist"), None),
            P(("geo", "dist"), None),
            P("dist", None),
            P("dist", None),
        ),
        out_specs=(P("dist", None), P("dist", None)),
        check_vma=False,
    )
```

time: 77.8 us -> 71.1 us (0.914)
  Pallas kernels: 77 us -> 70.3 us
    pallas_call x1, Pallas kernels: 64.5 us -> 57.7 us  [tile_sums(): pl.pallas_call(sums_kernel, out_shape=jax.ShapeDtypeStruct((SLOTS, CODE_R...]
where the time goes in v4:
time: 71.1 us; the launch traced here: 70.9 us
  Pallas kernels  70.3 us (99%)
    pallas_call x1, Pallas kernels, tile_sums(): pl.pallas_call(sums_kernel, out_shape=jax.ShapeDtypeStruct((SLOTS, CODE_R...  57.7 us
    pallas_call x1, Pallas kernels, blocks(): pl.pallas_call(blocks_kernel, out_shape=(jax.ShapeDtypeStruct((DB, TABLE_...  12.5 us

profile of v4, /device:TPU:1, one launch (start us, length us, event | category | flops | bytes accessed | tf_op | source)
XLA Modules:
  0.0 70.9 jit_solution(3093164904206113713)
XLA Ops:
  0.6 57.7 %tile_sums.1.slots = s16[120,136,128]{2,1,0:T(8,128)(2,1)S(1)} custom-call(s32[32,128]{1,0:T(8,128)} %bitcast.3, s32[32,128]{1,0:T(8,128)} %bitcast.4, bf16[48,7424]{1,0:T(8,128)(2,1)} %est_hbm.1, bf16[48,7424]{1,0:T(8,128)(2,1)} %fac_hbm.1, bf16[48,116]{1,0:T(8,128)(2,1)} %var_hbm.1), custom_call_target="tpu_custom_call" | custom-call | tf_op jit(solution)/shard_map/tile_sums/pallas_call | solution.py:371
  58.4 12.5 %district_blocks.1 = (f32[128,7424]{1,0:T(8,128)}, f32[13456,128]{1,0:T(8,128)}) custom-call(s16[120,136,128]{2,1,0:T(8,128)(2,1)S(1)} %tile_sums.1.slots), custom_call_target="tpu_custom_call" | custom-call | tf_op jit(solution)/shard_map/district_blocks/pallas_call | solution.py:469

commit v5 on v4

--- a/solution.py
+++ b/solution.py
@@ -26,11 +26,21 @@
 AHEAD = 3
 
 
-def sums_kernel(idx_hbm, wgt_hbm, est_hbm, fac_hbm, var_hbm, out,
+GROUP = 8
+CROWS = 120
+
+
+def decode(slots, slot):
+    code = slots[slot, 0:DB, :].astype(jnp.int32).astype(jnp.float32)
+    e = slots[slot, DB:CODE_ROWS, :].astype(jnp.int32).astype(jnp.float32)
+    return code * (jnp.exp2(e[0:1, :]) * (1.0 / STEPS))
+
+
+def sums_kernel(idx_hbm, wgt_hbm, est_hbm, fac_hbm, var_hbm, out, outer,
                 idx, wgt, est, fac, var, in_sem,
                 pk, varp, table, weight, block, sums, coded,
                 ready, own_sem, pk_send, pk_recv, row_send, row_recv, fwd_send, fwd_recv,
-                tile_send, slot_recv, right_send, left_send, core_send, core_recv):
+                tile_send, slot_recv, right_send, left_send, core_send, core_recv, loading, paired):
     g = lax.axis_index("geo")
     d = lax.axis_index("dist")
     me = g * DIST + d
@@ -313,23 +323,59 @@
         if n == 6:
             many_of(from_dist, 0, 4, 8)
     many_of(from_sides, 0, 0, 8)
-    many_of(from_dist, 1, 0, 8)
+    many_of(from_dist, 1, 0, 4)
     many_of(from_far, 0, 0, 8)
-    many_of(from_sides, 1, 0, 8)
-    many_of(from_far, 1, 0, 8)
+    many_of(from_dist, 1, 4, 8)
 
     def wait_slots(sem, n):
         ref = out.at[pl.ds(0, n)]
         pltpu.make_async_copy(ref, ref, sem).wait()
-    odd_side = jnp.where(c == 1, 1, 0)
-    for kind in range(2):
-        @pl.when(odd_side == 1 - kind)
+
+    def from_core(kind):
+        @pl.when(c == 1 - kind)
         def _():
             wait_slots(core_recv.at[kind], 4 * 8)
 
-        @pl.when(odd_side == kind)
+        @pl.when(c == kind)
         def _():
             wait_slots(core_recv.at[kind], 4 * 7)
+    from_core(0)
+
+    def load_tile(t, _):
+        loading[pl.ds(pl.multiple_of(t * DB, DB), DB), :] = decode(out, t)
+        return 0
+    lax.fori_loop(0, TABLE_TILES, load_tile, 0)
+    paired[...] = jnp.zeros_like(paired)
+    low_row = lax.broadcasted_iota(jnp.int32, (TABLE_TILES, LANES), 1) < RANK
+    low_full = lax.broadcasted_iota(jnp.int32, (LANES, LANES), 1) < RANK
+
+    def group(grp, _):
+        for k in range(GROUP):
+            rows = loading[pl.ds(grp * GROUP + k, TABLE_TILES, stride=DB), :]
+            turned = pltpu.roll(rows, RANK, axis=1)
+            paired[k, pl.ds(0, TABLE_TILES, stride=2), :] = jnp.where(low_row, rows, turned)
+            paired[k, pl.ds(1, TABLE_TILES, stride=2), :] = jnp.where(low_row, turned, rows)
+        for k in range(GROUP):
+            full = paired[k]
+            hi = full.astype(jnp.bfloat16)
+            lo = (full - hi.astype(jnp.float32)).astype(jnp.bfloat16)
+            mixed = jnp.where(low_full, hi, lo)
+            left = jnp.concatenate([mixed, mixed], axis=1)
+            right = jnp.concatenate([hi, lo], axis=1)
+            product = lax.dot_general(left, right, (((1,), (1,)), ((), ())), preferred_element_type=jnp.float32)
+            outer[pl.ds(pl.multiple_of((grp * GROUP + k) * CROWS, 8), CROWS), :] = product[0:CROWS, :]
+
+        @pl.when(grp < 8)
+        def _():
+            from_sides(1, grp)
+
+        @pl.when(grp >= 8)
+        def _():
+            from_far(1, grp - 8)
+        return 0
+    lax.fori_loop(0, DB // GROUP, group, 0)
+
+    from_core(1)
     wait_slots(core_send.at[0], 4 * PER_X)
     wait_slots(right_send.at[0], PER_X)
     wait_slots(left_send.at[0], PER_X)
@@ -370,9 +416,10 @@
     dma = pltpu.SemaphoreType.DMA
     return pl.pallas_call(
         sums_kernel,
-        out_shape=jax.ShapeDtypeStruct((SLOTS, CODE_ROWS, LANES), jnp.int16),
+        out_shape=(jax.ShapeDtypeStruct((SLOTS, CODE_ROWS, LANES), jnp.int16),
+                   jax.ShapeDtypeStruct((DB * CROWS, LANES), jnp.float32)),
         in_specs=[hbm] * 5,
-        out_specs=vmem,
+        out_specs=(vmem, vmem),
         scratch_shapes=[
             pltpu.VMEM((INTER, DB), jnp.int32),
             pltpu.VMEM((INTER, DB), jnp.int32),
@@ -389,56 +436,20 @@
             pltpu.VMEM((2, HALF, CODE_ROWS, LANES), jnp.int16),
             pltpu.SemaphoreType.REGULAR, dma((2,)), dma((1,)), dma((1,)), dma((2,)), dma((8,)), dma((2,)), dma((8,)),
             dma((2,)), dma((SLOTS,)), dma((2,)), dma((2,)), dma((1,)), dma((2,)),
+            pltpu.VMEM((TABLE_TILES * DB, LANES), jnp.float32),
+            pltpu.VMEM((GROUP, LANES, LANES), jnp.float32),
         ],
-        compiler_params=pltpu.CompilerParams(has_side_effects=True, collective_id=0, vmem_limit_bytes=40 * 2**20),
+        compiler_params=pltpu.CompilerParams(has_side_effects=True, collective_id=0, vmem_limit_bytes=32 * 2**20),
         name="tile_sums",
     )(idx, wgt, est, fac, var)
 
 
-GROUP = 8
-CROWS = 120
 CHUNK = 4
 
 
-def blocks_kernel(slots, marg_hbm, cov_hbm, loading, marg, noise, paired, outer, flat, marg_sem, cov_sem):
-    def decode(slot):
-        code = slots[slot, 0:DB, :].astype(jnp.int32).astype(jnp.float32)
-        e = slots[slot, DB:CODE_ROWS, :].astype(jnp.int32).astype(jnp.float32)
-        return code * (jnp.exp2(e[0:1, :]) * (1.0 / STEPS))
-
-    for t in range(TABLE_TILES):
-        marg[:, t * LANES:(t + 1) * LANES] = decode(CHIPS + t)
-    out_marg = pltpu.make_async_copy(marg, marg_hbm, marg_sem)
-    out_marg.start()
-
-    noise[...] = jnp.transpose(decode(HI) + decode(LO) * (1.0 / 256.0))
-
-    for t in range(TABLE_TILES):
-        loading[t * DB:(t + 1) * DB, :] = decode(t)
-
-    paired[...] = jnp.zeros_like(paired)
-    lane_row = lax.broadcasted_iota(jnp.int32, (TABLE_TILES, LANES), 1)
-    lane_full = lax.broadcasted_iota(jnp.int32, (LANES, LANES), 1)
+def blocks_kernel(slots, outer, marg_hbm, cov_hbm, marg, noise, flat, marg_sem, cov_sem):
+    noise[...] = jnp.transpose(decode(slots, HI) + decode(slots, LO) * (1.0 / 256.0))
     sub = lax.broadcasted_iota(jnp.int32, (LANES, LANES), 0)
-
-    def group(grp, _):
-        for k in range(GROUP):
-            rows = loading[pl.ds(grp * GROUP + k, TABLE_TILES, stride=DB), :]
-            turned = pltpu.roll(rows, RANK, axis=1)
-            low = lane_row < RANK
-            paired[k, pl.ds(0, TABLE_TILES, stride=2), :] = jnp.where(low, rows, turned)
-            paired[k, pl.ds(1, TABLE_TILES, stride=2), :] = jnp.where(low, turned, rows)
-        for k in range(GROUP):
-            full = paired[k]
-            hi = full.astype(jnp.bfloat16)
-            lo = (full - hi.astype(jnp.float32)).astype(jnp.bfloat16)
-            mixed = jnp.where(lane_full < RANK, hi, lo)
-            left = jnp.concatenate([mixed, mixed], axis=1)
-            right = jnp.concatenate([hi, lo], axis=1)
-            product = lax.dot_general(left, right, (((1,), (1,)), ((), ())), preferred_element_type=jnp.float32)
-            outer[pl.ds(pl.multiple_of((grp * GROUP + k) * CROWS, 8), CROWS), :] = product[0:CROWS, :]
-        return 0
-    lax.fori_loop(0, DB // GROUP, group, 0)
 
     span = CHUNK * AGES
 
@@ -458,11 +469,15 @@
         cov_copy(n).start()
         return 0
     lax.fori_loop(0, AGES // CHUNK, ages, 0)
+    for t in range(TABLE_TILES):
+        marg[:, t * LANES:(t + 1) * LANES] = decode(slots, CHIPS + t)
+    out_marg = pltpu.make_async_copy(marg, marg_hbm, marg_sem)
+    out_marg.start()
     pltpu.make_async_copy(flat, cov_hbm, cov_sem).wait()
     out_marg.wait()
 
 
-def blocks(slots):
+def blocks(slots, outer):
     vmem = pl.BlockSpec(memory_space=pltpu.VMEM)
     hbm = pl.BlockSpec(memory_space=pltpu.MemorySpace.HBM)
     dma = pltpu.SemaphoreType.DMA
@@ -470,27 +485,24 @@
         blocks_kernel,
         out_shape=(jax.ShapeDtypeStruct((DB, TABLE_TILES * LANES), jnp.float32),
                    jax.ShapeDtypeStruct((AGES * AGES, DB), jnp.float32)),
-        in_specs=[vmem],
+        in_specs=[vmem, vmem],
         out_specs=(hbm, hbm),
         scratch_shapes=[
-            pltpu.VMEM((TABLE_TILES * DB, LANES), jnp.float32),
             pltpu.VMEM((DB, TABLE_TILES * LANES), jnp.float32),
             pltpu.VMEM((DB, LANES), jnp.float32),
-            pltpu.VMEM((GROUP, LANES, LANES), jnp.float32),
-            pltpu.VMEM((DB * CROWS, LANES), jnp.float32),
             pltpu.VMEM((AGES * AGES, DB), jnp.float32),
             dma(()), dma(()),
         ],
-        compiler_params=pltpu.CompilerParams(vmem_limit_bytes=48 * 2**20),
+        compiler_params=pltpu.CompilerParams(vmem_limit_bytes=24 * 2**20),
         name="district_blocks",
-    )(slots)
+    )(slots, outer)
     return marg, cov.T
 
 
 def shards(estimates, factors, variances, intersection_tracts, intersection_weights):
     keep = lambda a: pltpu.with_memory_space_constraint(a, pltpu.MemorySpace.HBM)
-    slots = tile_sums(keep(intersection_tracts.T), keep(intersection_weights.T), keep(estimates), keep(factors), keep(variances))
-    return blocks(slots)
+    slots, outer = tile_sums(keep(intersection_tracts.T), keep(intersection_weights.T), keep(estimates), keep(factors), keep(variances))
+    return blocks(slots, outer)
 
 
 def solution(mesh):

time: 71.1 us -> 66.3 us (0.932)
  Pallas kernels: 70.3 us -> 65.5 us
    pallas_call x1, Pallas kernels: 12.5 us -> 6.39 us  [blocks(): pl.pallas_call(blocks_kernel, out_shape=(jax.ShapeDtypeStruct((DB, TABLE_...]
    pallas_call x1, Pallas kernels: 57.7 us -> 59.1 us  [tile_sums(): pl.pallas_call(sums_kernel, out_shape=(jax.ShapeDtypeStruct((SLOTS, CODE_...]
where the time goes in v5:
time: 66.3 us; the launch traced here: 66.1 us
  Pallas kernels  65.5 us (99%)
    pallas_call x1, Pallas kernels, tile_sums(): pl.pallas_call(sums_kernel, out_shape=(jax.ShapeDtypeStruct((SLOTS, CODE_...  59.1 us
    pallas_call x1, Pallas kernels, blocks(): pl.pallas_call(blocks_kernel, out_shape=(jax.ShapeDtypeStruct((DB, TABLE_...  6.39 us

profile of v5, /device:TPU:1, one launch (start us, length us, event | category | flops | bytes accessed | tf_op | source)
XLA Modules:
  0.0 66.1 jit_solution(3639594745928823293)
XLA Ops:
  0.6 59.1 %tile_sums.1 = (s16[120,136,128]{2,1,0:T(8,128)(2,1)S(1)}, f32[15360,128]{1,0:T(8,128)S(1)}) custom-call(s32[32,128]{1,0:T(8,128)} %bitcast.3, s32[32,128]{1,0:T(8,128)} %bitcast.4, bf16[48,7424]{1,0:T(8,128)(2,1)} %est_hbm.1, bf16[48,7424]{1,0:T(8,128)(2,1)} %fac_hbm.1, bf16[48,116]{1,0:T(8,128)(2,1)} %var_hbm.1), custom_call_target="tpu_custom_call" | custom-call | tf_op jit(solution)/shard_map/tile_sums/pallas_call | solution.py:417
  59.7 6.4 %district_blocks.1 = (f32[128,7424]{1,0:T(8,128)}, f32[13456,128]{1,0:T(8,128)}) custom-call(s16[120,136,128]{2,1,0:T(8,128)(2,1)S(1)} %get-tuple-element.6.slots, f32[15360,128]{1,0:T(8,128)S(1)} %get-tuple-element.7.outer), custom_call_target="tpu_custom_call" | custom-call | tf_op jit(solution)/shard_map/district_blocks/pallas_call | solution.py:484

commit v6 on v5

--- a/solution.py
+++ b/solution.py
@@ -28,6 +28,7 @@
 
 GROUP = 8
 CROWS = 120
+SPREAD = DB + 8
 
 
 def decode(slots, slot):
@@ -342,7 +343,7 @@
     from_core(0)
 
     def load_tile(t, _):
-        loading[pl.ds(pl.multiple_of(t * DB, DB), DB), :] = decode(out, t)
+        loading[pl.ds(pl.multiple_of(t * SPREAD, 8), DB), :] = decode(out, t)
         return 0
     lax.fori_loop(0, TABLE_TILES, load_tile, 0)
     paired[...] = jnp.zeros_like(paired)
@@ -351,7 +352,7 @@
 
     def group(grp, _):
         for k in range(GROUP):
-            rows = loading[pl.ds(grp * GROUP + k, TABLE_TILES, stride=DB), :]
+            rows = loading[pl.ds(grp * GROUP + k, TABLE_TILES, stride=SPREAD), :]
             turned = pltpu.roll(rows, RANK, axis=1)
             paired[k, pl.ds(0, TABLE_TILES, stride=2), :] = jnp.where(low_row, rows, turned)
             paired[k, pl.ds(1, TABLE_TILES, stride=2), :] = jnp.where(low_row, turned, rows)
@@ -436,7 +437,7 @@
             pltpu.VMEM((2, HALF, CODE_ROWS, LANES), jnp.int16),
             pltpu.SemaphoreType.REGULAR, dma((2,)), dma((1,)), dma((1,)), dma((2,)), dma((8,)), dma((2,)), dma((8,)),
             dma((2,)), dma((SLOTS,)), dma((2,)), dma((2,)), dma((1,)), dma((2,)),
-            pltpu.VMEM((TABLE_TILES * DB, LANES), jnp.float32),
+            pltpu.VMEM((TABLE_TILES * SPREAD, LANES), jnp.float32),
             pltpu.VMEM((GROUP, LANES, LANES), jnp.float32),
         ],
         compiler_params=pltpu.CompilerParams(has_side_effects=True, collective_id=0, vmem_limit_bytes=32 * 2**20),

time: 66.3 us -> 65.6 us (0.989)
  Pallas kernels: 65.5 us -> 64.8 us
where the time goes in v6:
time: 65.6 us; the launch traced here: 65.4 us
  Pallas kernels  64.8 us (99%)
    pallas_call x1, Pallas kernels, tile_sums(): pl.pallas_call(sums_kernel, out_shape=(jax.ShapeDtypeStruct((SLOTS, CODE_...  58.4 us
    pallas_call x1, Pallas kernels, blocks(): pl.pallas_call(blocks_kernel, out_shape=(jax.ShapeDtypeStruct((DB, TABLE_...  6.39 us

profile of v6, /device:TPU:1, one launch (start us, length us, event | category | flops | bytes accessed | tf_op | source)
XLA Modules:
  0.0 65.4 jit_solution(11186892787072615548)
XLA Ops:
  0.6 58.4 %tile_sums.1 = (s16[120,136,128]{2,1,0:T(8,128)(2,1)S(1)}, f32[15360,128]{1,0:T(8,128)S(1)}) custom-call(s32[32,128]{1,0:T(8,128)} %bitcast.3, s32[32,128]{1,0:T(8,128)} %bitcast.4, bf16[48,7424]{1,0:T(8,128)(2,1)} %est_hbm.1, bf16[48,7424]{1,0:T(8,128)(2,1)} %fac_hbm.1, bf16[48,116]{1,0:T(8,128)(2,1)} %var_hbm.1), custom_call_target="tpu_custom_call" | custom-call | tf_op jit(solution)/shard_map/tile_sums/pallas_call | solution.py:418
  59.1 6.4 %district_blocks.1 = (f32[128,7424]{1,0:T(8,128)}, f32[13456,128]{1,0:T(8,128)}) custom-call(s16[120,136,128]{2,1,0:T(8,128)(2,1)S(1)} %get-tuple-element.6.slots, f32[15360,128]{1,0:T(8,128)S(1)} %get-tuple-element.7.outer), custom_call_target="tpu_custom_call" | custom-call | tf_op jit(solution)/shard_map/district_blocks/pallas_call | solution.py:485

commit v7 on v6

--- a/solution.py
+++ b/solution.py
@@ -437,7 +437,7 @@
             pltpu.VMEM((2, HALF, CODE_ROWS, LANES), jnp.int16),
             pltpu.SemaphoreType.REGULAR, dma((2,)), dma((1,)), dma((1,)), dma((2,)), dma((8,)), dma((2,)), dma((8,)),
             dma((2,)), dma((SLOTS,)), dma((2,)), dma((2,)), dma((1,)), dma((2,)),
-            pltpu.VMEM((TABLE_TILES * SPREAD, LANES), jnp.float32),
+            pltpu.VMEM(((TABLE_TILES + 6) * SPREAD, LANES), jnp.float32),
             pltpu.VMEM((GROUP, LANES, LANES), jnp.float32),
         ],
         compiler_params=pltpu.CompilerParams(has_side_effects=True, collective_id=0, vmem_limit_bytes=32 * 2**20),

time: 65.6 us -> 65.6 us (level)
  no operation moved by 1% of the time
where the time goes in v7:
time: 65.6 us; the launch traced here: 65.4 us
  Pallas kernels  64.8 us (99%)
    pallas_call x1, Pallas kernels, tile_sums(): pl.pallas_call(sums_kernel, out_shape=(jax.ShapeDtypeStruct((SLOTS, CODE_...  58.4 us
    pallas_call x1, Pallas kernels, blocks(): pl.pallas_call(blocks_kernel, out_shape=(jax.ShapeDtypeStruct((DB, TABLE_...  6.39 us

profile of v7, /device:TPU:1, one launch (start us, length us, event | category | flops | bytes accessed | tf_op | source)
XLA Modules:
  0.0 65.4 jit_solution(14069019436802096511)
XLA Ops:
  0.6 58.4 %tile_sums.1 = (s16[120,136,128]{2,1,0:T(8,128)(2,1)S(1)}, f32[15360,128]{1,0:T(8,128)S(1)}) custom-call(s32[32,128]{1,0:T(8,128)} %bitcast.3, s32[32,128]{1,0:T(8,128)} %bitcast.4, bf16[48,7424]{1,0:T(8,128)(2,1)} %est_hbm.1, bf16[48,7424]{1,0:T(8,128)(2,1)} %fac_hbm.1, bf16[48,116]{1,0:T(8,128)(2,1)} %var_hbm.1), custom_call_target="tpu_custom_call" | custom-call | tf_op jit(solution)/shard_map/tile_sums/pallas_call | solution.py:418
  59.1 6.4 %district_blocks.1 = (f32[128,7424]{1,0:T(8,128)}, f32[13456,128]{1,0:T(8,128)}) custom-call(s16[120,136,128]{2,1,0:T(8,128)(2,1)S(1)} %get-tuple-element.6.slots, f32[15360,128]{1,0:T(8,128)S(1)} %get-tuple-element.7.outer), custom_call_target="tpu_custom_call" | custom-call | tf_op jit(solution)/shard_map/district_blocks/pallas_call | solution.py:485
